TPU v7x, 512 devices: a whole 4x4x16 slice. The times are simulated.
512 devices in a mesh: seq: 64 (over z, x), batch: 8 (over y, core).
Axes of the slice: x: 4, y: 4, z: 16, core: 2. Of those that a mesh axis runs over, the one named last changes fastest.
Arguments:
- inputs: bfloat16 [8, 8192, 256], P('batch', 'seq'), may hold values from -6 to 6
- cotangent: bfloat16 [8, 8192, 256], P('batch', 'seq'), may hold values from -6 to 6
- decay_rate: float32 [32, 256], replicated, as said below
- rotation: float32 [32, 256], replicated, may hold values from -3.140625 to 3.140625
- readout: float32 [2, 32, 256], replicated, may hold values from -1.5 to 1.5
- skip_gain: float32 [256], replicated, may hold values from -4 to 4
- projection: bfloat16 [256, 256], replicated, may hold values from -0.375 to 0.375
Outputs:
- outputs: bfloat16 [8, 8192, 256], P('batch', 'seq')
- input_grad: bfloat16 [8, 8192, 256], P('batch', 'seq')
- proj_grad: float32 [256, 256], replicated
- readout_grad: float32 [2, 32, 256], replicated
- skip_grad: float32 [256], replicated
Inputs may be any that keep to these rules, and one draw needn't show every extreme that they name: `decay_rate`: every decay rate is positive.
All inputs are finite; a program needn't handle non-finite values.
Results may differ from a plain program's by a relative error of at most 0.004.
Values sent between devices are 32-bit elements; how exact they have to be, the bound alone decides.
A program may use at most 128 MiB of HBM per device.

v0:
```python
from functools import partial
import math

import jax
import jax.numpy as jnp
from jax import lax
from jax.sharding import PartitionSpec as P

BLOCK = 16


PRECISE = lax.Precision.HIGHEST


def entering(value, axis, join, neutral, backward):
    count, mine = (lax.axis_size(axis), lax.axis_index(axis))
    pieces = jax.tree.map(lambda part: lax.all_gather(part, axis), value)
    if backward:
        pieces = jax.tree.map(lambda part: part[::-1], pieces)
        mine = count - 1 - mine
    so_far = jax.tree.map(
        lambda part, zero: jnp.full_like(part, 0) + jnp.asarray(zero, part.dtype), value, neutral
    )

    def step(position, so_far):
        longer = join(so_far, jax.tree.map(lambda part: part[position], pieces))
        return jax.tree.map(lambda new, old: jnp.where(position < mine, new, old), longer, so_far)

    return lax.fori_loop(0, count - 1, step, so_far)


def contract(form, table, data):
    return jnp.einsum(form, table, data, precision=PRECISE)


def complex_mul(left_re, left_im, right_re, right_im):
    return (left_re * right_re - left_im * right_im, left_re * right_im + left_im * right_re)


def powers(decay_rate, rotation, block_len):
    exponents = jnp.arange(block_len + 1).astype(jnp.float32)[:, None, None]
    magnitude = jnp.exp(-decay_rate[None] * exponents)
    return (
        magnitude * jnp.cos(rotation[None] * exponents),
        magnitude * jnp.sin(rotation[None] * exponents),
    )


def kernels(pow_re, pow_im, readout, in_gain, block_len):
    kernel = jnp.sum(
        in_gain * (readout[0] * pow_re[:block_len] - readout[1] * pow_im[:block_len]), axis=1
    )
    positions = jnp.arange(block_len)
    lag_index = positions[:, None] - positions[None, :]
    toeplitz = jnp.where(
        (lag_index >= 0)[:, :, None], kernel[jnp.clip(lag_index, 0, block_len - 1)], 0.0
    )
    diag_table = (lag_index[:, :, None] == positions[None, None, :]).astype(jnp.float32)
    return (toeplitz, diag_table)


def carry_across(span_re, span_im, value_re, value_im, backward):
    zeros_state = jnp.zeros_like(value_re)
    ones_state = jnp.ones_like(value_re)

    def chain_pairs(earlier, later):
        mult_re, mult_im = complex_mul(earlier[0], earlier[1], later[0], later[1])
        moved_re, moved_im = complex_mul(later[0], later[1], earlier[2], earlier[3])
        return (mult_re, mult_im, moved_re + later[2], moved_im + later[3])

    result = entering(
        (span_re, span_im, value_re, value_im),
        "seq",
        chain_pairs,
        (ones_state, zeros_state, zeros_state, zeros_state),
        backward,
    )
    return (result[2], result[3])


def shards(inputs, cotangent, decay_rate, rotation, readout, skip_gain, projection):
    samples = inputs[0]
    tangent = cotangent[0]
    length, channels = samples.shape
    block_len = BLOCK
    blocks = length // block_len
    pow_re, pow_im = powers(decay_rate, rotation, block_len)
    in_gain = jnp.sqrt(-jnp.expm1(-2.0 * decay_rate))
    toeplitz, diag_table = kernels(pow_re, pow_im, readout, in_gain, block_len)
    step_re, step_im = (pow_re[block_len], pow_im[block_len])
    zeros_state = jnp.zeros_like(decay_rate)
    ones_state = jnp.ones_like(decay_rate)
    segments = samples.astype(jnp.float32).reshape(blocks, block_len, channels)
    fill_re = in_gain * contract("snh,bsh->bnh", pow_re[block_len - 1 :: -1], segments)
    fill_im = in_gain * contract("snh,bsh->bnh", pow_im[block_len - 1 :: -1], segments)

    def advance(carried, fills):
        run_re, run_im, power_re, power_im = carried
        new_re, new_im = complex_mul(step_re, step_im, run_re, run_im)
        next_power_re, next_power_im = complex_mul(step_re, step_im, power_re, power_im)
        return (
            (new_re + fills[0], new_im + fills[1], next_power_re, next_power_im),
            (run_re, run_im, power_re, power_im),
        )

    final, history = lax.scan(
        advance, (zeros_state, zeros_state, ones_state, zeros_state), (fill_re, fill_im)
    )
    end_re, end_im, span_re, span_im = final
    before_re, before_im, power_re, power_im = history
    enter_re, enter_im = carry_across(span_re, span_im, end_re, end_im, False)
    inject_re, inject_im = complex_mul(power_re, power_im, enter_re, enter_im)
    mixed_re, mixed_im = complex_mul(
        readout[0], readout[1], before_re + inject_re, before_im + inject_im
    )
    mixed_out = contract("jnh,bnh->bjh", pow_re[1:], mixed_re) - contract(
        "jnh,bnh->bjh", pow_im[1:], mixed_im
    )
    mixed_out = mixed_out + contract("jsh,bsh->bjh", toeplitz, segments) + skip_gain * segments
    mixed_out = mixed_out.reshape(length, channels)
    hidden = jax.nn.gelu(mixed_out, approximate=True).astype(jnp.bfloat16)
    outputs = (
        samples.astype(jnp.float32)
        + jnp.dot(hidden, projection, preferred_element_type=jnp.float32)
    ).astype(jnp.bfloat16)
    proj_part = jnp.einsum("th,tk->hk", hidden, tangent, preferred_element_type=jnp.float32)
    hidden_back = jnp.einsum("tk,hk->th", tangent, projection, preferred_element_type=jnp.float32)
    _, gelu_back = jax.vjp(partial(jax.nn.gelu, approximate=True), mixed_out)
    mixed_grad = gelu_back(hidden_back)[0]
    grad_segments = mixed_grad.reshape(blocks, block_len, channels)
    fresh_re = contract("jnh,bjh->bnh", pow_re[:block_len], grad_segments)
    fresh_im = contract("jnh,bjh->bnh", pow_im[:block_len], grad_segments)

    def retreat(carried, fresh):
        run_re, run_im = carried
        new_re, new_im = complex_mul(step_re, step_im, run_re, run_im)
        return ((new_re + fresh[0], new_im + fresh[1]), (run_re, run_im))

    start, after = lax.scan(retreat, (zeros_state, zeros_state), (fresh_re, fresh_im), reverse=True)
    leave_re, leave_im = carry_across(span_re, span_im, start[0], start[1], True)
    inject_re, inject_im = complex_mul(power_re[::-1], power_im[::-1], leave_re, leave_im)
    next_re = after[0] + inject_re
    next_im = after[1] + inject_im
    weighted_re, weighted_im = complex_mul(
        readout[0], readout[1], in_gain * next_re, in_gain * next_im
    )
    grad_within = contract("snh,bnh->bsh", pow_re[block_len:0:-1], weighted_re) - contract(
        "snh,bnh->bsh", pow_im[block_len:0:-1], weighted_im
    )
    grad_within = (
        grad_within + contract("jsh,bjh->bsh", toeplitz, grad_segments) + skip_gain * grad_segments
    )
    input_grad = (grad_within.reshape(length, channels) + tangent.astype(jnp.float32)).astype(
        jnp.bfloat16
    )
    lead_re = contract("snh,bsh->bnh", pow_re[block_len:0:-1], segments)
    lead_im = contract("snh,bsh->bnh", pow_im[block_len:0:-1], segments)
    prod_re, prod_im = complex_mul(lead_re, lead_im, next_re, next_im)
    acc_re = in_gain * jnp.sum(prod_re, axis=0)
    acc_im = in_gain * jnp.sum(prod_im, axis=0)
    correlation = contract("bjh,bsh->jsh", grad_segments, segments)
    lag_sum = jnp.einsum("jsh,jsd->dh", correlation, diag_table, precision=PRECISE)
    acc_re = acc_re + in_gain * jnp.einsum(
        "dnh,dh->nh", pow_re[:block_len], lag_sum, precision=PRECISE
    )
    acc_im = acc_im + in_gain * jnp.einsum(
        "dnh,dh->nh", pow_im[:block_len], lag_sum, precision=PRECISE
    )
    readout_part = jnp.stack([acc_re, -acc_im])
    skip_part = jnp.sum(mixed_grad * segments.reshape(length, channels), axis=0)
    params = channels * channels + 2 * decay_rate.shape[0] * channels + channels
    ceiling = math.sqrt(params)
    proj_sum, readout_sum, skip_sum = lax.psum(
        (proj_part, readout_part, skip_part), ("seq", "batch")
    )
    squares = (
        jnp.sum(proj_sum * proj_sum)
        + jnp.sum(readout_sum * readout_sum)
        + jnp.sum(skip_sum * skip_sum)
    )
    factor = jnp.minimum(1.0, ceiling / (jnp.sqrt(squares) + 1e-06))
    proj_grad = factor * proj_sum
    readout_grad = factor * readout_sum
    skip_grad = factor * skip_sum
    return (outputs[None], input_grad[None], proj_grad, readout_grad, skip_grad)


def solution(mesh):
    placed = (P("batch", "seq", None), P("batch", "seq", None), P(), P(), P(), P(), P())
    return jax.shard_map(
        shards,
        mesh=mesh,
        in_specs=placed,
        out_specs=(P("batch", "seq", None), P("batch", "seq", None), P(), P(), P()),
        check_vma=False,
    )
```

profile of v0, /device:TPU:1, one launch (start us, length us, event | category | flops | bytes accessed | tf_op | source)
XLA Modules:
  0.0 1589.8 jit_solution(11231814899570196803)
XLA Ops:
  16.1 12.4 fusion.8
  35.1 7.1 fusion.67
  42.2 3.8 rev.33
  46.0 3.8 fusion.69
  49.8 2.2 copy.200
  52.1 3.8 rev.32
  55.9 3.9 fusion.68
  59.7 2.2 copy.198
  66.8 16.6 %while.78 = (s32[]{:T(128)}, f32[32,256]{1,0:T(8,128)S(1)}, f32[32,256]{1,0:T(8,128)S(1)}, f32[32,256]{1,0:T(8,128)S(1)}, f32[32,256]{1,0:T(8,128)S(1)}, /*index...) while((s32[]{:T(128)}, f32[32,256]{1,0:T(8,128)S(1)}, ...), condition=%wide.region_1.2_spmd.clone, body=%wide.region_0.0_spmd.clone.sunk | while | flops 180227 | bytes 655533 | solution.py:106
  92.3 3.4 copy.210
  96.3 4.4 fusion.14
  102.9 118.6 %all-gather.13.cloned.1.call-done = f32[2048,256]{1,0:T(8,128)} async-done(((f32[32,256]{1,0:T(8,128)}), f32[2048,256]{1,0:T(8,128)}) %all-gather.13.cloned.1.call-update) | async-done | bytes 2097168 | tf_op jit(solution)/shard_map/all_gather | solution.py:17
  221.5 140.5 %all-gather.15.cloned.1.call-done = f32[2048,256]{1,0:T(8,128)} async-done(((f32[32,256]{1,0:T(8,128)}), f32[2048,256]{1,0:T(8,128)}) %all-gather.15.cloned.1.call-update) | async-done | bytes 2097168 | tf_op jit(solution)/shard_map/all_gather | solution.py:17
  362.0 139.9 %all-gather.17.cloned.1.call-done = f32[2048,256]{1,0:T(8,128)} async-done(((f32[32,256]{1,0:T(8,128)}), f32[2048,256]{1,0:T(8,128)}) %all-gather.17.cloned.1.call-update) | async-done | bytes 2097168 | tf_op jit(solution)/shard_map/all_gather | solution.py:17
  501.9 139.8 %all-gather.19.cloned.1.call-done = f32[2048,256]{1,0:T(8,128)} async-done(((f32[32,256]{1,0:T(8,128)}), f32[2048,256]{1,0:T(8,128)}) %all-gather.19.cloned.1.call-update) | async-done | bytes 2097168 | tf_op jit(solution)/shard_map/all_gather | solution.py:17
  641.7 54.0 %while.79 = (s32[]{:T(128)}, f32[32,256]{1,0:T(8,128)S(1)}, f32[32,256]{1,0:T(8,128)S(1)}, s32[]{:T(128)}, f32[64,32,256]{2,1,0:T(8,128)}, /*index=5*/f32[64,32,...) while((s32[]{:T(128)}, f32[32,256]{1,0:T(8,128)S(1)}, ...), condition=%wide.region_3.4_spmd.clone, body=%wide.region_2.3_spmd.clone.sunk | while | flops 98308 | bytes 262277 | solution.py:29
  698.5 2.3 copy.203
  700.8 6.6 fusion.58
  707.4 2.2 copy.205
  709.6 2.3 copy.204
  711.9 5.7 fusion.56
  717.6 2.2 copy.206
  723.6 2.2 copy.213
  725.8 4.9 convolution_bitcast_fusion.2
  730.7 2.8 convolution_bitcast_fusion.1
  733.6 2.4 copy.217
  736.0 2.3 copy.218
  739.7 11.5 while.80
  752.5 3.8 rev.41
  756.3 3.8 fusion.73
  760.1 2.2 copy.228
  762.4 3.8 rev.40
  766.2 3.8 fusion.72
  770.0 2.2 copy.226
  772.3 3.2 rev.35
  775.5 3.1 rev.36
  778.6 4.9 fusion.12
  785.7 110.5 %psum.23 = f32[256]{0:T(256)S(1)} all-reduce(f32[256]{0:T(256)S(1)} %copy-done.35), channel_id=1, replica_groups=mesh['seq'=64,'batch'=8] {'seq','batch'}, use_global_device_ids=true, to_apply=%region_16.17 | all-reduce | flops 256 | bytes 2048 | tf_op jit(solution)/shard_map/psum | solution.py:173
  899.5 3.4 convolution_bitcast_fusion
  904.5 2.5 fusion.63
  907.1 2.5 fusion.60
  911.5 117.3 %all-gather.23.cloned.1.call-done = f32[2048,256]{1,0:T(8,128)} async-done(((f32[32,256]{1,0:T(8,128)}), f32[2048,256]{1,0:T(8,128)}) %all-gather.23.cloned.1.call-update) | async-done | bytes 2097168 | tf_op jit(solution)/shard_map/all_gather | solution.py:17
  1028.7 3.3 rev.38
  1032.0 53.3 %while.81 = (s32[]{:T(128)}, f32[32,256]{1,0:T(8,128)S(1)}, f32[32,256]{1,0:T(8,128)S(1)}, s32[]{:T(128)}, f32[64,32,256]{2,1,0:T(8,128)}, /*index=5*/f32[64,32,...) while((s32[]{:T(128)}, f32[32,256]{1,0:T(8,128)S(1)}, ...), condition=%wide.region_8.9_spmd.clone, body=%wide.region_7.8_spmd.clone.sunk | while | flops 98308 | bytes 262277 | solution.py:29
  1090.4 4.4 fusion.70
  1094.8 2.3 copy.221
  1097.5 4.4 fusion.71
  1107.8 466.1 %all-reduce.3.cloned.1.call-done = (f32[256,256]{1,0:T(8,128)}, f32[2,32,256]{2,1,0:T(8,128)}) async-done(((f32[256,256]{1,0:T(8,128)}, f32[2,32,256]{2,1,0:T(8,128)}), (f32[256,256]{1,0:T(8,128)}, f32[2,32,256]{2,1,0:T(8,128)})) %all-reduce.3.cloned.1.call-update) | async-done | bytes 327696 | tf_op jit(solution)/shard_map/psum | solution.py:173
  (322 shorter events, 200.1 us)
Async XLA Ops:
  7.2 715.0 %copy-start = (bf16[256,256]{1,0:T(8,128)(2,1)S(1)}, bf16[256,256]{1,0:T(8,128)(2,1)}, u32[]{:S(2)}) copy-start(bf16[256,256]{1,0:T(8,128)(2,1)} %param.21) | copy-start | bytes 393220
  7.2 214.3 %all-gather.13.cloned.1.call-start = ((), (), s32[]{:S(2)}) async-start(), calls=%async_computation | async-start | bytes 2129920 | tf_op jit(solution)/shard_map/all_gather | solution.py:17
  8.9 7.2 copy-start.14
  13.9 683.9 %copy-start.18 = (f32[32,256]{1,0:T(8,128)}, f32[32,256]{1,0:T(8,128)S(1)}, u32[]{:S(2)}) copy-start(f32[32,256]{1,0:T(8,128)S(1)} %get-tuple-element.914) | copy-start | bytes 98308
  13.9 683.9 %copy-start.19 = (f32[32,256]{1,0:T(8,128)}, f32[32,256]{1,0:T(8,128)S(1)}, u32[]{:S(2)}) copy-start(f32[32,256]{1,0:T(8,128)S(1)} %get-tuple-element.915) | copy-start | bytes 98308
  28.5 1.6 copy-start.1
  83.3 0.6 copy-start.8
  83.4 0.7 copy-start.9
  83.4 1.4 copy-start.6
  83.4 2.1 copy-start.7
  84.0 278.0 %all-gather.15.cloned.1.call-start = ((), (), s32[]{:S(2)}) async-start(), calls=%async_computation.1 | async-start | bytes 2129920 | tf_op jit(solution)/shard_map/all_gather | solution.py:17
  84.7 417.2 %all-gather.17.cloned.1.call-start = ((), (), s32[]{:S(2)}) async-start(), calls=%async_computation.2 | async-start | bytes 2129920 | tf_op jit(solution)/shard_map/all_gather | solution.py:17
  85.5 556.2 %all-gather.19.cloned.1.call-start = ((), (), s32[]{:S(2)}) async-start(), calls=%async_computation.3 | async-start | bytes 2129920 | tf_op jit(solution)/shard_map/all_gather | solution.py:17
  86.1 823.6 %all-gather.21.cloned.1.call-start = ((), (), s32[]{:S(2)}) async-start(), calls=%async_computation.4 | async-start | bytes 2129920 | tf_op jit(solution)/shard_map/all_gather | solution.py:17
  95.8 0.5 copy-start.29
  711.9 7.9 copy-start.20
  711.9 7.9 copy-start.31
  711.9 10.3 copy-start.27
  721.5 0.7 copy-start.25
  725.8 4.9 copy-start.3
  751.2 0.6 copy-start.10
  751.3 0.7 copy-start.11
  751.9 276.8 %all-gather.23.cloned.1.call-start = ((), (), s32[]{:S(2)}) async-start(), calls=%async_computation.5 | async-start | bytes 2129920 | tf_op jit(solution)/shard_map/all_gather | solution.py:17
  752.5 821.5 %all-reduce.3.cloned.1.call-start = ((), (), s32[]{:S(2)}) async-start(), calls=%async_computation.6 | async-start | bytes 655360 | tf_op jit(solution)/shard_map/psum | solution.py:173
  775.4 3.1 copy-start.30
  778.6 7.1 copy-start.35
  778.6 118.3 %copy-start.26 = (f32[8,16,256]{2,1,0:T(8,128)S(1)}, f32[8,16,256]{2,1,0:T(8,128)}, u32[]{:S(2)}) copy-start(f32[8,16,256]{2,1,0:T(8,128)} %copy-done.25) | copy-start | bytes 393220
  896.2 6.6 copy-start.33
  899.5 5.0 copy-start.2
  1028.7 56.7 %copy-start.12 = (f32[8,32,256]{2,1,0:T(8,128)S(1)}, f32[8,32,256]{2,1,0:T(8,128)}, u32[]{:S(2)}) copy-start(f32[8,32,256]{2,1,0:T(8,128)} %get-tuple-element.542) | copy-start | bytes 786436
  1028.7 56.7 %copy-start.13 = (f32[8,32,256]{2,1,0:T(8,128)S(1)}, f32[8,32,256]{2,1,0:T(8,128)}, u32[]{:S(2)}) copy-start(f32[8,32,256]{2,1,0:T(8,128)} %get-tuple-element.548) | copy-start | bytes 786436
  1028.7 56.7 %copy-start.16 = (f32[256,32,8]{0,1,2:T(8,128)S(1)}, f32[256,32,8]{0,1,2:T(8,128)}, u32[]{:S(2)}) copy-start(f32[256,32,8]{0,1,2:T(8,128)} %copy.228) | copy-start | bytes 786436
  1028.7 56.7 %copy-start.17 = (f32[256,32,8]{0,1,2:T(8,128)S(1)}, f32[256,32,8]{0,1,2:T(8,128)}, u32[]{:S(2)}) copy-start(f32[256,32,8]{0,1,2:T(8,128)} %copy.226) | copy-start | bytes 786436
  1085.4 5.0 copy-start.5
  1094.8 2.8 copy-start.4
  1097.5 7.7 copy-start.15
  1097.5 7.7 copy-start.23
  1101.9 5.2 copy-start.21
  1101.9 5.2 copy-start.22
  1101.9 5.2 copy-start.24
  1101.9 5.2 copy-start.32
  1101.9 5.3 copy-start.28
  1103.5 478.6 %copy-start.34 = (f32[256]{0:T(256)S(1)}, f32[256]{0:T(256)}, u32[]{:S(2)}) copy-start(f32[256]{0:T(256)} %copy-done.33) | copy-start | bytes 3076
Sparse Core Ops, SparseCore 0:
  84.1 137.3 all-gather.12
  225.0 136.9 all-gather.14
  365.0 136.9 all-gather.16
  504.7 136.9 all-gather.18
  752.0 136.9 all-gather.20
  891.8 136.8 all-gather.22
  1107.2 466.6 all-reduce.2
where the time goes:
time: 1610 us; the launch traced here: 1590 us
  waiting for transfers between devices  1120 us (70%)
  other arithmetic  175 us (11%)
  blocking collectives  111 us (7%)
  local copies, waits for them, and re-layouts  91.7 us (6%)
  matrix products  67.6 us (4%)
  between operations  16.8 us (1%)
    all_gather x6, waiting for transfers between devices, entering(): pieces = jax.tree.map(lambda part: lax.all_gather(part, axis), value)  656 us
    psum x1, waiting for transfers between devices, shards(): lax.psum((proj_part, readout_part, skip_part), ('seq', 'batch'))  466 us
    psum x1, blocking collectives, shards(): lax.psum((proj_part, readout_part, skip_part), ('seq', 'batch'))  111 us
    select_n x126, other arithmetic, step(): jnp.where(position < mine, new, old)  104 us
    dot_general x13, matrix products, contract(): return jnp.einsum(form, table, data, precision=PRECISE)  56.8 us
  transfers between devices with their start and end apart: 7, of which 6 were waited for; matrix products, arithmetic and copies ran while one was open for 4% of the time, Pallas kernels for 0%

commit v1 on v0

v1 whole, which is shorter than its diff:
```python
import math

import jax
import jax.numpy as jnp
import numpy as np
from jax import lax
from jax.experimental import pallas as pl
from jax.experimental.pallas import tpu as pltpu
from jax.sharding import PartitionSpec as P

MESH = pl.DeviceIdType.MESH
F32 = jnp.float32
STATES, CHANNELS, RUN = 32, 256, 128
GROUP = 8
BLOCKS = 8
OWNERS = 32

TURN_HI = 6.28125
TURN_MID = round((2 * math.pi - TURN_HI) * 2**20) / 2**20
TURN_LO = 2 * math.pi - TURN_HI - TURN_MID
GELU_SCALE = math.sqrt(2 / math.pi)
GELU_CUBE = 0.044715
CEILING = math.sqrt(CHANNELS * CHANNELS + 2 * STATES * CHANNELS + CHANNELS)


def cmul(a, b):
    return a[0] * b[0] - a[1] * b[1], a[0] * b[1] + a[1] * b[0]


def decay_power(decay, rotation, times):
    angle = rotation * float(times)
    if times > 1:
        turns = jnp.floor(angle * (0.5 / math.pi) + 0.5)
        angle = ((angle - turns * TURN_HI) - turns * TURN_MID) - turns * TURN_LO
    size = jnp.exp(decay * -float(times))
    return size * jnp.cos(angle), size * jnp.sin(angle)


def entry_gain(decay):
    y = 2.0 * decay
    series = 1.0 - y * (1.0 / 8)
    for k in (7, 6, 5, 4, 3, 2):
        series = 1.0 - y * (1.0 / k) * series
    return jnp.sqrt(jnp.where(y < 0.25, y * series, 1.0 - jnp.exp(-y)))


def put_pieces(ref, value):
    re, im = value
    for p in range(GROUP):
        rows, cols = slice(8 * (p // 2), 8 * (p // 2) + 8), slice(128 * (p % 2), 128 * (p % 2) + 128)
        ref[p, 0:8, :] = re[rows, cols]
        ref[p, 8:16, :] = im[rows, cols]


def get_pieces(ref):
    def part(lo):
        return jnp.concatenate(
            [
                jnp.concatenate([ref[2 * n, lo : lo + 8, :], ref[2 * n + 1, lo : lo + 8, :]], axis=1)
                for n in range(4)
            ],
            axis=0,
        )

    return part(0), part(8)


def load(ref, i):
    return ref[i, 0:8, :], ref[i, 8:16, :]


def store(ref, i, value):
    ref[i, 0:8, :] = value[0]
    ref[i, 8:16, :] = value[1]


def kernel(
    x_ref, cot_ref, decay_ref, rot_ref, read_ref, skip_ref, proj_ref,
    out_ref, ig_ref, pg_ref, rg_ref, sg_ref,
    xf, gf, mix, hb, il,
    lam_s, cof_s, l128, l1024,
    e_buf, o_buf, t_buf, r1f, r2f, hin, r1b, r2b, lin,
    pb, gb, ra1p, ra1g, a2s, ra2, pc, ra3, full,
    ssem, rsem,
):
    s, b = lax.axis_index("seq"), lax.axis_index("batch")
    g, blk = lax.rem(s, GROUP), lax.div(s, GROUP)
    y, c = lax.div(b, 2), lax.rem(b, 2)
    me = lax.div(g, 4) * 16 + lax.rem(g, 4) * 4 + y

    def in_block(k):
        return {"seq": blk * GROUP + lax.rem(g + k, GROUP), "batch": b}

    def across(k):
        return {"seq": lax.rem(blk + k, BLOCKS) * GROUP + g, "batch": b}

    def owner(k):
        o = lax.rem(me + k, OWNERS)
        seq = blk * GROUP + lax.div(o, 16) * 4 + lax.div(lax.rem(o, 16), 4)
        return o, {"seq": seq, "batch": lax.rem(o, 4) * 2 + c}

    other = {"seq": s, "batch": y * 2 + (1 - c)}

    barrier = pltpu.get_barrier_semaphore()
    partners = [across(k) for k in range(1, BLOCKS)]
    partners += [owner(k)[1] for k in range(1, OWNERS)] + [other]
    partners_n = len(partners)
    for device in partners:
        pl.semaphore_signal(barrier, inc=1, device_id=device, device_id_type=MESH)

    def copy(src, dst, n, device):
        return pltpu.make_async_remote_copy(
            src_ref=src, dst_ref=dst, send_sem=ssem.at[n], recv_sem=rsem.at[n],
            device_id=device, device_id_type=MESH,
        )

    decay, rot = decay_ref[...], rot_ref[...]
    gain = entry_gain(decay)
    lam = decay_power(decay, rot, 1)
    put_pieces(l128, decay_power(decay, rot, RUN))
    put_pieces(l1024, decay_power(decay, rot, RUN * GROUP))
    lam_s[0], lam_s[1] = lam
    cof_s[0] = gain * read_ref[0]
    cof_s[1] = gain * read_ref[1]
    xf[...] = x_ref[...].astype(F32)
    row_id = lax.broadcasted_iota(jnp.int32, (8, CHANNELS), 0)
    zero = jnp.zeros((STATES, CHANNELS), F32)

    def sweep(carry, body, backward=False):
        def step(i, carry):
            first = RUN - 8 - 8 * i if backward else 8 * i
            first = pl.multiple_of(first, 8)
            return body(first, carry)

        return lax.fori_loop(0, RUN // 8, step, carry)

    order = tuple(range(8))

    def fwd_local(first, carry):
        lam_re, lam_im = lam_s[0], lam_s[1]
        cof_re, cof_im = cof_s[0], cof_s[1]
        rows = xf[pl.ds(first, 8), :]
        re, im = carry
        acc = jnp.zeros((8, CHANNELS), F32)
        for j in order:
            re, im = lam_re * re - lam_im * im + rows[j : j + 1, :], lam_re * im + lam_im * re
            total = jnp.sum(cof_re * re - cof_im * im, axis=0, keepdims=True)
            acc = jnp.where(row_id == j, total, acc)
        mix[pl.ds(first, 8), :] = acc + rows * skip_ref[...]
        return re, im

    re, im = sweep((zero, zero), fwd_local)
    put_pieces(e_buf, (gain * re, gain * im))
    hb[...] = lax.dot_general(
        cot_ref[...], proj_ref[...], (((1,), (1,)), ((), ())), preferred_element_type=F32
    )
    pl.semaphore_wait(barrier, partners_n)

    sends = []

    def scatter(buf, dst, n):
        dst[g] = buf[g]
        for k in range(1, GROUP):
            p = lax.rem(g + k, GROUP)
            copy(buf.at[p], dst.at[g], n, in_block(k)).start()
        sends.append((buf.at[pl.ds(0, GROUP - 1)], n))

    def spread(src, dst, n):
        dst[blk] = src[...]
        for k in range(1, BLOCKS):
            copy(src, dst.at[blk], n, across(k)).start()
        sends.append((dst.at[pl.ds(0, BLOCKS - 1)], n))

    def arrive(ref, n):
        copy(ref, ref, n, other).wait_recv()

    def block_total(r1, turn):
        step = load(l128, g)
        total = load(r1, turn[0])
        for i in turn[1:]:
            moved = cmul(step, total)
            nxt = load(r1, i)
            total = moved[0] + nxt[0], moved[1] + nxt[1]
        return total

    def entering(r1, r2, buf, turn, backward):
        step, leap = load(l128, g), load(l1024, g)
        state = (jnp.zeros((8, 128), F32), jnp.zeros((8, 128), F32))
        for i in turn:
            moved, nxt = cmul(leap, state), load(r2, i)
            use = (i > blk) if backward else (i < blk)
            state = tuple(jnp.where(use, m + v, old) for m, v, old in zip(moved, nxt, state))
        for i in turn:
            store(buf, i, state)
            moved, nxt = cmul(step, state), load(r1, i)
            state = moved[0] + nxt[0], moved[1] + nxt[1]

    up, down = tuple(range(8)), tuple(range(7, -1, -1))
    seven = pl.ds(0, 7)

    scatter(e_buf, r1f, 0)
    arrive(r1f.at[seven], 0)
    t = block_total(r1f, up)
    t_buf[0, 0:8, :], t_buf[0, 8:16, :] = t
    spread(t_buf.at[0], r2f, 1)
    arrive(r2f.at[seven], 1)
    entering(r1f, r2f, o_buf.at[0], up, False)
    scatter(o_buf.at[0], hin, 2)
    arrive(hin.at[seven], 2)

    enter = get_pieces(hin)
    carried = cmul((read_ref[0], read_ref[1]), enter)

    def fwd_inject(first, carry):
        lam_re, lam_im = lam_s[0], lam_s[1]
        re, im = carry
        acc = jnp.zeros((8, CHANNELS), F32)
        for j in order:
            re, im = lam_re * re - lam_im * im, lam_re * im + lam_im * re
            acc = jnp.where(row_id == j, jnp.sum(re, axis=0, keepdims=True), acc)
        mix[pl.ds(first, 8), :] = mix[pl.ds(first, 8), :] + acc
        return re, im

    sweep(carried, fwd_inject)

    mixed = mix[...]
    square = mixed * mixed
    tanh = jnp.tanh(GELU_SCALE * (mixed + GELU_CUBE * (mixed * square)))
    half = 0.5 * (1.0 + tanh)
    hidden = (mixed * half).astype(jnp.bfloat16)
    slope = half + (0.5 * mixed) * (1.0 - tanh * tanh) * (
        GELU_SCALE * (1.0 + (3.0 * GELU_CUBE) * square)
    )
    grad = hb[...] * slope
    gf[...] = grad
    part = lax.dot_general(
        hidden, cot_ref[...], (((0,), (0,)), ((), ())), preferred_element_type=F32
    )
    for half_id in range(2):
        for o in range(OWNERS):
            pb[half_id, o] = part[8 * o : 8 * o + 8, 128 * half_id : 128 * half_id + 128]
    copy(pb.at[1 - c], ra1p, 3, other).start()
    sends.append((pb.at[0], 3))

    def bwd_local(first, carry):
        lam_re, lam_im = lam_s[0], lam_s[1]
        rows, xs = gf[pl.ds(first, 8), :], xf[pl.ds(first, 8), :]
        re, im, sum_re, sum_im = carry
        for j in reversed(order):
            re, im = lam_re * re - lam_im * im + rows[j : j + 1, :], lam_re * im + lam_im * re
            sum_re = sum_re + xs[j : j + 1, :] * re
            sum_im = sum_im + xs[j : j + 1, :] * im
        return re, im, sum_re, sum_im

    re, im, sum_re, sum_im = sweep((zero, zero, zero, zero), bwd_local, True)
    put_pieces(e_buf.at[pl.ds(GROUP, GROUP)], (re, im))
    scatter(e_buf.at[pl.ds(GROUP, GROUP)], r1b, 4)
    lam = lam_s[0], lam_s[1]
    extra = cmul(cmul(lam, (re, im)), get_pieces(hin))
    read_re = gain * sum_re + extra[0]
    read_im = -(gain * sum_im + extra[1])
    skip_part = jnp.sum(gf[...] * xf[...], axis=0, keepdims=True)
    for half_id in range(2):
        cols = slice(128 * half_id, 128 * half_id + 128)
        for n in range(4):
            gb[half_id, n] = read_re[8 * n : 8 * n + 8, cols]
            gb[half_id, 4 + n] = read_im[8 * n : 8 * n + 8, cols]
        gb[half_id, 8] = jnp.where(row_id[:, :128] == 0, skip_part[:, cols], 0.0)
    copy(gb.at[1 - c], ra1g, 5, other).start()
    sends.append((gb.at[0], 5))
    a2s[...] = jnp.zeros_like(a2s)
    arrive(ra1p, 3)
    for o in range(OWNERS):
        a2s[o, 0:8, :] = pb[c, o] + ra1p[o]
    arrive(ra1g, 5)
    for o in range(9):
        a2s[o, 8:16, :] = gb[c, o] + ra1g[o]
    ra2[me] = a2s[me]
    for k in range(1, OWNERS):
        o, device = owner(k)
        copy(a2s.at[o], ra2.at[me], 6, device).start()
    sends.append((ra2.at[pl.ds(0, OWNERS - 1)], 6))

    out_ref[...] = (
        xf[...] + jnp.dot(hidden, proj_ref[...], preferred_element_type=F32)
    ).astype(jnp.bfloat16)

    arrive(r1b.at[seven], 4)
    t = block_total(r1b, down)
    t_buf[1, 0:8, :], t_buf[1, 8:16, :] = t
    spread(t_buf.at[1], r2b, 7)

    def bwd_read(first, carry):
        lam_re, lam_im = lam_s[0], lam_s[1]
        cof_re, cof_im = cof_s[0], cof_s[1]
        rows = gf[pl.ds(first, 8), :]
        re, im = carry
        acc = jnp.zeros((8, CHANNELS), F32)
        for j in reversed(order):
            re, im = lam_re * re - lam_im * im + rows[j : j + 1, :], lam_re * im + lam_im * re
            total = jnp.sum(cof_re * re - cof_im * im, axis=0, keepdims=True)
            acc = jnp.where(row_id == j, total, acc)
        il[pl.ds(first, 8), :] = acc + rows * skip_ref[...]
        return re, im

    sweep((zero, zero), bwd_read, True)
    il[...] = il[...] + cot_ref[...].astype(F32)

    arrive(ra2.at[pl.ds(0, OWNERS - 1)], 6)
    total = ra2[0]
    for o in range(1, OWNERS):
        total = total + ra2[o]
    pc[0] = total
    spread(pc.at[0], ra3, 8)

    arrive(r2b.at[seven], 7)
    entering(r1b, r2b, o_buf.at[1], down, True)
    scatter(o_buf.at[1], lin, 9)

    arrive(ra3.at[seven], 8)
    total = ra3[0]
    for o in range(1, BLOCKS):
        total = total + ra3[o]
    full[c, me] = total
    for k in range(1, OWNERS):
        copy(full.at[c, me], full.at[c, me], 10, owner(k)[1]).start()
    sends.append((ra2.at[pl.ds(0, OWNERS - 1)], 10))

    arrive(lin.at[seven], 9)
    carried = cmul((cof_s[0], cof_s[1]), get_pieces(lin))

    def bwd_inject(first, carry):
        lam_re, lam_im = lam_s[0], lam_s[1]
        re, im = carry
        acc = jnp.zeros((8, CHANNELS), F32)
        for j in reversed(order):
            re, im = lam_re * re - lam_im * im, lam_re * im + lam_im * re
            acc = jnp.where(row_id == j, jnp.sum(re, axis=0, keepdims=True), acc)
        il[pl.ds(first, 8), :] = il[pl.ds(first, 8), :] + acc
        return re, im

    sweep(carried, bwd_inject, True)
    ig_ref[...] = il[...].astype(jnp.bfloat16)

    arrive(full.at[0, pl.ds(0, OWNERS - 1)], 10)
    copy(full.at[c], full.at[c], 11, other).start()
    sends.append((full.at[0], 11))
    arrive(full.at[0], 11)

    squares = jnp.zeros((16, 128), F32)
    for half_id in range(2):
        for o in range(OWNERS):
            v = full[half_id, o]
            squares = squares + v * v
    norm = jnp.sqrt(jnp.sum(jnp.sum(squares, axis=0, keepdims=True), axis=1, keepdims=True))
    factor = jnp.minimum(1.0, CEILING / (norm + 1e-06))
    for half_id in range(2):
        cols = slice(128 * half_id, 128 * half_id + 128)
        for o in range(OWNERS):
            pg_ref[8 * o : 8 * o + 8, cols] = full[half_id, o, 0:8, :] * factor
        for n in range(4):
            rg_ref[0, 8 * n : 8 * n + 8, cols] = full[half_id, n, 8:16, :] * factor
            rg_ref[1, 8 * n : 8 * n + 8, cols] = full[half_id, 4 + n, 8:16, :] * factor
        sg_ref[:, cols] = full[half_id, 8, 8:9, :] * factor
    for ref, n in sends:
        copy(ref, ref, n, other).wait_send()


def shards(inputs, cotangent, decay_rate, rotation, readout, skip_gain, projection):
    bf16 = jnp.bfloat16
    row, state = (RUN, CHANNELS), (2, STATES, CHANNELS)
    pieces = (GROUP, 16, 128)
    vmem = pl.BlockSpec(memory_space=pltpu.VMEM)
    shapes = [row] * 5 + [state, state, pieces, pieces]
    shapes += [(2 * GROUP, 16, 128), (2,) + pieces, (2, 16, 128)] + [pieces] * 6
    shapes += [(2, OWNERS, 8, 128), (2, 9, 8, 128), (OWNERS, 8, 128), (9, 8, 128)]
    shapes += [(OWNERS, 16, 128), (OWNERS, 16, 128), (1, 16, 128), pieces, (2, OWNERS, 16, 128)]
    outs = pl.pallas_call(
        kernel,
        out_shape=(
            jax.ShapeDtypeStruct(row, bf16),
            jax.ShapeDtypeStruct(row, bf16),
            jax.ShapeDtypeStruct((CHANNELS, CHANNELS), F32),
            jax.ShapeDtypeStruct(state, F32),
            jax.ShapeDtypeStruct((1, CHANNELS), F32),
        ),
        in_specs=[vmem] * 7,
        out_specs=[vmem] * 5,
        scratch_shapes=[pltpu.VMEM(shape, F32) for shape in shapes]
        + [pltpu.SemaphoreType.DMA((12,)), pltpu.SemaphoreType.DMA((12,))],
        compiler_params=pltpu.CompilerParams(
            collective_id=0, has_side_effects=True, vmem_limit_bytes=32 << 20
        ),
        name="layer",
    )(
        inputs[0], cotangent[0], decay_rate, rotation, readout,
        skip_gain.reshape(1, CHANNELS), projection,
    )
    return outs[0][None], outs[1][None], outs[2], outs[3], outs[4].reshape(CHANNELS)


def solution(mesh):
    split = P("batch", "seq", None)
    return jax.shard_map(
        shards,
        mesh=mesh,
        in_specs=(split, split, P(), P(), P(), P(), P()),
        out_specs=(split, split, P(), P(), P()),
        check_vma=False,
    )
```

time: 1610 us -> 70.7 us (0.04); the launches traced: 1590 us -> 70.2 us
  waiting for transfers between devices: 1120 us -> 0 us
  other arithmetic: 175 us -> 0 us
  blocking collectives: 111 us -> 0 us
  local copies, waits for them, and re-layouts: 91.7 us -> 8.76 us
  matrix products: 67.6 us -> 0 us
  Pallas kernels: 0 us -> 60.8 us
  between operations: 16.8 us -> 0.66 us
    all_gather x6 -> x0, waiting for transfers between devices: 656 us -> none  [entering(): pieces = jax.tree.map(lambda part: lax.all_gather(part, axis), value)]
    psum x1 -> x0, waiting for transfers between devices: 466 us -> none  [shards(): lax.psum((proj_part, readout_part, skip_part), ('seq', 'batch'))]
    psum x1 -> x0, blocking collectives: 111 us -> none  [shards(): lax.psum((proj_part, readout_part, skip_part), ('seq', 'batch'))]
    select_n x127 -> x0, other arithmetic: 105 us -> none  [the longest x126 104 us: step(): jnp.where(position < mine, new, old)]
    dot_general x19 -> x0, matrix products: 67.6 us -> none  [the longest x13 56.8 us: contract(): return jnp.einsum(form, table, data, precision=PRECISE)]
    pallas_call x0 -> x1, Pallas kernels: none -> 60.8 us  [shards(): pl.pallas_call(kernel, out_shape=(jax.ShapeDtypeStruct(row, bf16), jax.Sh...]
    rev x8 -> x0, local copies, waits for them, and re-layouts: 26.7 us -> none  [the longest x4 11.5 us: entering(): pieces = jax.tree.map(lambda part: part[::-1], pieces)]
    dot_general x10 -> x0, local copies, waits for them, and re-layouts: 21.6 us -> none  [contract(): return jnp.einsum(form, table, data, precision=PRECISE)]
  transfers between devices with their start and end apart: 7 -> 0, of which waited for: 6 -> 0; matrix products, arithmetic and copies ran while one was open for 4% -> 0% of each run, Pallas kernels for 0% -> 0%
where the time goes in v1:
time: 70.7 us; the launch traced here: 70.2 us
  Pallas kernels  60.8 us (86%)
  local copies, waits for them, and re-layouts  8.76 us (12%)
    pallas_call x1, Pallas kernels, shards(): pl.pallas_call(kernel, out_shape=(jax.ShapeDtypeStruct(row, bf16), jax.Sh...  60.8 us
    unnamed x19, local copies, waits for them, and re-layouts  8.76 us

profile of v1, /device:TPU:1, one launch (start us, length us, event | category | flops | bytes accessed | tf_op | source)
XLA Modules:
  0.0 70.2 jit_solution(10530039814999899561)
XLA Ops:
  0.6 0.0 copy-start.6
  0.6 0.7 copy-done.6
  1.3 0.0 copy-start
  1.3 0.9 %copy-done = bf16[256,256]{1,0:T(8,128)(2,1)S(1)} copy-done((bf16[256,256]{1,0:T(8,128)(2,1)S(1)}, bf16[256,256]{1,0:T(8,128)(2,1)}, u32[]{:S(2)}) %copy-start) | copy-done | bytes 131096
  2.2 0.0 copy-start.1
  2.2 0.8 %copy-done.1 = bf16[1,128,256]{2,1,0:T(8,128)(2,1)S(1)} copy-done((bf16[1,128,256]{2,1,0:T(8,128)(2,1)S(1)}, bf16[1,128,256]{2,1,0:T(8,128)(2,1)}, u32[]{:S(2)}) %copy-start.1) | copy-done | bytes 65560
  3.1 0.0 copy-start.2
  3.1 0.8 %copy-done.2 = bf16[1,128,256]{2,1,0:T(8,128)(2,1)S(1)} copy-done((bf16[1,128,256]{2,1,0:T(8,128)(2,1)S(1)}, bf16[1,128,256]{2,1,0:T(8,128)(2,1)}, u32[]{:S(2)}) %copy-start.2) | copy-done | bytes 65560
  3.9 0.0 copy-start.3
  3.9 0.8 %copy-done.3 = f32[2,32,256]{2,1,0:T(8,128)S(1)} copy-done((f32[2,32,256]{2,1,0:T(8,128)S(1)}, f32[2,32,256]{2,1,0:T(8,128)}, u32[]{:S(2)}) %copy-start.3) | copy-done | bytes 65560
  4.7 0.0 copy-start.4
  4.7 0.8 %copy-done.4 = f32[32,256]{1,0:T(8,128)S(1)} copy-done((f32[32,256]{1,0:T(8,128)S(1)}, f32[32,256]{1,0:T(8,128)}, u32[]{:S(2)}) %copy-start.4) | copy-done | bytes 32792
  5.5 0.0 copy-start.5
  5.5 0.8 %copy-done.5 = f32[32,256]{1,0:T(8,128)S(1)} copy-done((f32[32,256]{1,0:T(8,128)S(1)}, f32[32,256]{1,0:T(8,128)}, u32[]{:S(2)}) %copy-start.5) | copy-done | bytes 32792
  6.3 60.8 %layer.1 = (bf16[128,256]{1,0:T(8,128)(2,1)S(1)}, bf16[128,256]{1,0:T(8,128)(2,1)S(1)}, f32[256,256]{1,0:T(8,128)S(1)}, f32[2,32,256]{2,1,0:T(8,128)S(1)}, f32[1,256]{1,0:T(1,128)S(1)}) custom-call(bf16[128,256]{1,0:T(8,128)(2,1)S(1)} %bitcast.8, bf16[128,256]{1,0:T(8,128)(2,1)S(1)} %bitcast.9, f32[32,256]{1,0:T(8,128)S(1)} %copy-done.4, ...), custom_call_target="tpu_custom_call" | custom-call | tf_op jit(solution)/shard_map/layer/pallas_call | solution.py:378
  67.1 0.6 copy.17
  67.7 0.6 copy.18
  68.3 0.7 copy.19
  69.0 0.6 copy.20
  69.7 0.6 copy.21
Async XLA Ops:
  0.6 0.7 copy-start.6
  1.3 0.9 %copy-start = (bf16[256,256]{1,0:T(8,128)(2,1)S(1)}, bf16[256,256]{1,0:T(8,128)(2,1)}, u32[]{:S(2)}) copy-start(bf16[256,256]{1,0:T(8,128)(2,1)} %proj_ref.1) | copy-start | bytes 393220
  2.2 0.8 %copy-start.1 = (bf16[1,128,256]{2,1,0:T(8,128)(2,1)S(1)}, bf16[1,128,256]{2,1,0:T(8,128)(2,1)}, u32[]{:S(2)}) copy-start(bf16[1,128,256]{2,1,0:T(8,128)(2,1)} %param.7) | copy-start | bytes 196612
  3.1 0.8 %copy-start.2 = (bf16[1,128,256]{2,1,0:T(8,128)(2,1)S(1)}, bf16[1,128,256]{2,1,0:T(8,128)(2,1)}, u32[]{:S(2)}) copy-start(bf16[1,128,256]{2,1,0:T(8,128)(2,1)} %param.8) | copy-start | bytes 196612
  3.9 0.8 %copy-start.3 = (f32[2,32,256]{2,1,0:T(8,128)S(1)}, f32[2,32,256]{2,1,0:T(8,128)}, u32[]{:S(2)}) copy-start(f32[2,32,256]{2,1,0:T(8,128)} %read_ref.1) | copy-start | bytes 196612
  4.7 0.8 %copy-start.4 = (f32[32,256]{1,0:T(8,128)S(1)}, f32[32,256]{1,0:T(8,128)}, u32[]{:S(2)}) copy-start(f32[32,256]{1,0:T(8,128)} %decay_ref.1) | copy-start | bytes 98308
  5.5 0.8 %copy-start.5 = (f32[32,256]{1,0:T(8,128)S(1)}, f32[32,256]{1,0:T(8,128)}, u32[]{:S(2)}) copy-start(f32[32,256]{1,0:T(8,128)} %rot_ref.1) | copy-start | bytes 98308

commit v2 on v1

--- a/solution.py
+++ b/solution.py
@@ -75,13 +75,14 @@
 
 
 def kernel(
+    x_hbm, cot_hbm, decay_hbm, rot_hbm, read_hbm, skip_hbm, proj_hbm,
+    out_ref, ig_ref, full,
     x_ref, cot_ref, decay_ref, rot_ref, read_ref, skip_ref, proj_ref,
-    out_ref, ig_ref, pg_ref, rg_ref, sg_ref,
     xf, gf, mix, hb, il,
     lam_s, cof_s, l128, l1024,
     e_buf, o_buf, t_buf, r1f, r2f, hin, r1b, r2b, lin,
-    pb, gb, ra1p, ra1g, a2s, ra2, pc, ra3, full,
-    ssem, rsem,
+    pb, gb, ra1p, ra1g, a2s, ra2, pc, ra3,
+    isem, ssem, rsem,
 ):
     s, b = lax.axis_index("seq"), lax.axis_index("batch")
     g, blk = lax.rem(s, GROUP), lax.div(s, GROUP)
@@ -100,6 +101,16 @@
         return o, {"seq": seq, "batch": lax.rem(o, 4) * 2 + c}
 
     other = {"seq": s, "batch": y * 2 + (1 - c)}
+
+    fetches = [
+        pltpu.make_async_copy(src, dst, isem.at[i])
+        for i, (src, dst) in enumerate(
+            [(decay_hbm, decay_ref), (rot_hbm, rot_ref), (read_hbm, read_ref), (x_hbm, x_ref),
+             (skip_hbm, skip_ref), (cot_hbm, cot_ref), (proj_hbm, proj_ref)]
+        )
+    ]
+    for fetch in fetches:
+        fetch.start()
 
     barrier = pltpu.get_barrier_semaphore()
     partners = [across(k) for k in range(1, BLOCKS)]
@@ -113,6 +124,9 @@
             src_ref=src, dst_ref=dst, send_sem=ssem.at[n], recv_sem=rsem.at[n],
             device_id=device, device_id_type=MESH,
         )
+
+    for fetch in fetches:
+        fetch.wait()
 
     decay, rot = decay_ref[...], rot_ref[...]
     gain = entry_gain(decay)
@@ -238,7 +252,9 @@
     )
     for half_id in range(2):
         for o in range(OWNERS):
-            pb[half_id, o] = part[8 * o : 8 * o + 8, 128 * half_id : 128 * half_id + 128]
+            for q in range(2):
+                row = 8 * o + 4 * q
+                pb[half_id, o, q] = part[row : row + 4, 128 * half_id : 128 * half_id + 128]
     copy(pb.at[1 - c], ra1p, 3, other).start()
     sends.append((pb.at[0], 3))
 
@@ -260,35 +276,40 @@
     read_re = gain * sum_re + extra[0]
     read_im = -(gain * sum_im + extra[1])
     skip_part = jnp.sum(gf[...] * xf[...], axis=0, keepdims=True)
+    gb[...] = jnp.zeros_like(gb)
     for half_id in range(2):
         cols = slice(128 * half_id, 128 * half_id + 128)
-        for n in range(4):
-            gb[half_id, n] = read_re[8 * n : 8 * n + 8, cols]
-            gb[half_id, 4 + n] = read_im[8 * n : 8 * n + 8, cols]
-        gb[half_id, 8] = jnp.where(row_id[:, :128] == 0, skip_part[:, cols], 0.0)
+        for o in range(OWNERS):
+            rows = (read_re if o < 16 else read_im)[2 * (o % 16) : 2 * (o % 16) + 2, cols]
+            gb[half_id, o, 0:2, :] = rows
+        gb[half_id, 0, 2:3, :] = skip_part[:, cols]
     copy(gb.at[1 - c], ra1g, 5, other).start()
     sends.append((gb.at[0], 5))
-    a2s[...] = jnp.zeros_like(a2s)
     arrive(ra1p, 3)
     for o in range(OWNERS):
-        a2s[o, 0:8, :] = pb[c, o] + ra1p[o]
-    arrive(ra1g, 5)
-    for o in range(9):
-        a2s[o, 8:16, :] = gb[c, o] + ra1g[o]
-    ra2[me] = a2s[me]
+        a2s[o, 0:2] = pb[c, o] + ra1p[o]
+    ra2[me, 0:2] = a2s[me, 0:2]
     for k in range(1, OWNERS):
         o, device = owner(k)
-        copy(a2s.at[o], ra2.at[me], 6, device).start()
-    sends.append((ra2.at[pl.ds(0, OWNERS - 1)], 6))
-
-    out_ref[...] = (
-        xf[...] + jnp.dot(hidden, proj_ref[...], preferred_element_type=F32)
-    ).astype(jnp.bfloat16)
+        copy(a2s.at[o, pl.ds(0, 2)], ra2.at[me, pl.ds(0, 2)], 6, device).start()
+    sends.append((ra1p.at[pl.ds(0, OWNERS - 1)], 6))
+    arrive(ra1g, 5)
+    for o in range(OWNERS):
+        a2s[o, 2] = gb[c, o] + ra1g[o]
+    ra2[me, 2] = a2s[me, 2]
+    for k in range(1, OWNERS):
+        o, device = owner(k)
+        copy(a2s.at[o, 2], ra2.at[me, 2], 12, device).start()
+    sends.append((ra1g.at[pl.ds(0, OWNERS - 1)], 12))
 
     arrive(r1b.at[seven], 4)
     t = block_total(r1b, down)
     t_buf[1, 0:8, :], t_buf[1, 8:16, :] = t
     spread(t_buf.at[1], r2b, 7)
+
+    out_ref[...] = (
+        xf[...] + jnp.dot(hidden, proj_ref[...], preferred_element_type=F32)
+    ).astype(jnp.bfloat16)
 
     def bwd_read(first, carry):
         lam_re, lam_im = lam_s[0], lam_s[1]
@@ -306,7 +327,8 @@
     sweep((zero, zero), bwd_read, True)
     il[...] = il[...] + cot_ref[...].astype(F32)
 
-    arrive(ra2.at[pl.ds(0, OWNERS - 1)], 6)
+    arrive(ra2.at[pl.ds(0, OWNERS - 1), pl.ds(0, 2)], 6)
+    arrive(ra2.at[pl.ds(0, OWNERS - 1), 2], 12)
     total = ra2[0]
     for o in range(1, OWNERS):
         total = total + ra2[o]
@@ -342,60 +364,106 @@
     sweep(carried, bwd_inject, True)
     ig_ref[...] = il[...].astype(jnp.bfloat16)
 
-    arrive(full.at[0, pl.ds(0, OWNERS - 1)], 10)
+    arrive(full.at[c, pl.ds(0, OWNERS - 1)], 10)
     copy(full.at[c], full.at[c], 11, other).start()
     sends.append((full.at[0], 11))
-    arrive(full.at[0], 11)
-
-    squares = jnp.zeros((16, 128), F32)
+    arrive(full.at[1 - c], 11)
+    for ref, n in sends:
+        copy(ref, ref, n, other).wait_send()
+
+
+def finish(
+    out_ref, ig_ref, full,
+    out_hbm, ig_hbm, pg_hbm, rg_hbm, sg_hbm,
+    pg_ref, rg_ref, sg_ref, sem,
+):
+    def write(src, dst, i):
+        done = pltpu.make_async_copy(src, dst, sem.at[i])
+        done.start()
+        return done
+
+    writes = [write(out_ref, out_hbm, 0), write(ig_ref, ig_hbm, 1)]
+    squares = jnp.zeros((3, 4, 128), F32)
     for half_id in range(2):
         for o in range(OWNERS):
             v = full[half_id, o]
             squares = squares + v * v
+    squares = squares[0] + squares[1] + squares[2]
     norm = jnp.sqrt(jnp.sum(jnp.sum(squares, axis=0, keepdims=True), axis=1, keepdims=True))
     factor = jnp.minimum(1.0, CEILING / (norm + 1e-06))
     for half_id in range(2):
         cols = slice(128 * half_id, 128 * half_id + 128)
         for o in range(OWNERS):
-            pg_ref[8 * o : 8 * o + 8, cols] = full[half_id, o, 0:8, :] * factor
-        for n in range(4):
-            rg_ref[0, 8 * n : 8 * n + 8, cols] = full[half_id, n, 8:16, :] * factor
-            rg_ref[1, 8 * n : 8 * n + 8, cols] = full[half_id, 4 + n, 8:16, :] * factor
-        sg_ref[:, cols] = full[half_id, 8, 8:9, :] * factor
-    for ref, n in sends:
-        copy(ref, ref, n, other).wait_send()
+            for q in range(2):
+                row = 8 * o + 4 * q
+                pg_ref[row : row + 4, cols] = full[half_id, o, q] * factor
+            row = 2 * (o % 16)
+            rg_ref[o // 16, row : row + 2, cols] = full[half_id, o, 2, 0:2, :] * factor
+        sg_ref[:, cols] = full[half_id, 0, 2, 2:3, :] * factor
+    writes += [write(pg_ref, pg_hbm, 2), write(rg_ref, rg_hbm, 3), write(sg_ref, sg_hbm, 4)]
+    for done in writes:
+        done.wait()
 
 
 def shards(inputs, cotangent, decay_rate, rotation, readout, skip_gain, projection):
     bf16 = jnp.bfloat16
-    row, state = (RUN, CHANNELS), (2, STATES, CHANNELS)
+    row, state, square = (RUN, CHANNELS), (2, STATES, CHANNELS), (CHANNELS, CHANNELS)
     pieces = (GROUP, 16, 128)
+    sums = (2, OWNERS, 3, 4, 128)
     vmem = pl.BlockSpec(memory_space=pltpu.VMEM)
+    hbm = pl.BlockSpec(memory_space=pltpu.HBM)
+    operands = [
+        pltpu.VMEM(row, bf16), pltpu.VMEM(row, bf16), pltpu.VMEM(state[1:], F32),
+        pltpu.VMEM(state[1:], F32), pltpu.VMEM(state, F32), pltpu.VMEM((1, CHANNELS), F32),
+        pltpu.VMEM(square, bf16),
+    ]
     shapes = [row] * 5 + [state, state, pieces, pieces]
     shapes += [(2 * GROUP, 16, 128), (2,) + pieces, (2, 16, 128)] + [pieces] * 6
-    shapes += [(2, OWNERS, 8, 128), (2, 9, 8, 128), (OWNERS, 8, 128), (9, 8, 128)]
-    shapes += [(OWNERS, 16, 128), (OWNERS, 16, 128), (1, 16, 128), pieces, (2, OWNERS, 16, 128)]
-    outs = pl.pallas_call(
+    shapes += [(2, OWNERS, 2, 4, 128), (2, OWNERS, 4, 128), (OWNERS, 2, 4, 128), (OWNERS, 4, 128)]
+    shapes += [sums[1:], sums[1:], (1, 3, 4, 128), (BLOCKS, 3, 4, 128)]
+    out, in_grad, total = pl.pallas_call(
         kernel,
         out_shape=(
             jax.ShapeDtypeStruct(row, bf16),
             jax.ShapeDtypeStruct(row, bf16),
-            jax.ShapeDtypeStruct((CHANNELS, CHANNELS), F32),
-            jax.ShapeDtypeStruct(state, F32),
-            jax.ShapeDtypeStruct((1, CHANNELS), F32),
+            jax.ShapeDtypeStruct(sums, F32),
         ),
-        in_specs=[vmem] * 7,
-        out_specs=[vmem] * 5,
-        scratch_shapes=[pltpu.VMEM(shape, F32) for shape in shapes]
-        + [pltpu.SemaphoreType.DMA((12,)), pltpu.SemaphoreType.DMA((12,))],
+        in_specs=[hbm] * 7,
+        out_specs=[vmem] * 3,
+        scratch_shapes=operands
+        + [pltpu.VMEM(shape, F32) for shape in shapes]
+        + [pltpu.SemaphoreType.DMA((7,)), pltpu.SemaphoreType.DMA((13,)), pltpu.SemaphoreType.DMA((13,))],
         compiler_params=pltpu.CompilerParams(
             collective_id=0, has_side_effects=True, vmem_limit_bytes=32 << 20
         ),
         name="layer",
     )(
-        inputs[0], cotangent[0], decay_rate, rotation, readout,
-        skip_gain.reshape(1, CHANNELS), projection,
+        *(
+            pltpu.with_memory_space_constraint(v, pltpu.HBM)
+            for v in (
+                inputs[0], cotangent[0], decay_rate, rotation, readout,
+                skip_gain.reshape(1, CHANNELS), projection,
+            )
+        )
     )
+    outs = pl.pallas_call(
+        finish,
+        out_shape=(
+            jax.ShapeDtypeStruct(row, bf16),
+            jax.ShapeDtypeStruct(row, bf16),
+            jax.ShapeDtypeStruct(square, F32),
+            jax.ShapeDtypeStruct(state, F32),
+            jax.ShapeDtypeStruct((1, CHANNELS), F32),
+        ),
+        in_specs=[vmem] * 3,
+        out_specs=[hbm] * 5,
+        scratch_shapes=[
+            pltpu.VMEM(square, F32), pltpu.VMEM(state, F32), pltpu.VMEM((1, CHANNELS), F32),
+            pltpu.SemaphoreType.DMA((5,)),
+        ],
+        compiler_params=pltpu.CompilerParams(vmem_limit_bytes=4 << 20),
+        name="finish",
+    )(out, in_grad, total)
     return outs[0][None], outs[1][None], outs[2], outs[3], outs[4].reshape(CHANNELS)
 
 

time: 70.7 us -> 60.6 us (0.86)
  local copies, waits for them, and re-layouts: 8.76 us -> 0 us
  Pallas kernels: 60.8 us -> 59.8 us
    unnamed x19 -> x0, local copies, waits for them, and re-layouts: 8.76 us -> none
    pallas_call x1, Pallas kernels: 60.8 us -> 58.8 us  [shards(): pl.pallas_call(kernel, out_shape=(jax.ShapeDtypeStruct(row, bf16), jax.Sh...]
    pallas_call x0 -> x1, Pallas kernels: none -> 1.01 us  [shards(): pl.pallas_call(finish, out_shape=(jax.ShapeDtypeStruct(row, bf16), jax.Sh...]
where the time goes in v2:
time: 60.6 us; the launch traced here: 60.4 us
  Pallas kernels  59.8 us (99%)
  between operations  0.64 us (1%)
    pallas_call x1, Pallas kernels, shards(): pl.pallas_call(kernel, out_shape=(jax.ShapeDtypeStruct(row, bf16), jax.Sh...  58.8 us

profile of v2, /device:TPU:1, one launch (start us, length us, event | category | flops | bytes accessed | tf_op | source)
XLA Modules:
  0.0 60.4 jit_solution(11787163152215449430)
XLA Ops:
  0.6 58.8 %layer.1 = (bf16[128,256]{1,0:T(8,128)(2,1)S(1)}, bf16[128,256]{1,0:T(8,128)(2,1)S(1)}, f32[2,32,3,4,128]{4,3,2,1,0:T(4,128)S(1)}) custom-call(bf16[128,256]{1,0:T(8,128)(2,1)} %bitcast.6, bf16[128,256]{1,0:T(8,128)(2,1)} %bitcast.7, f32[32,256]{1,0:T(8,128)} %decay_hbm.1, f32[32,256]{1,0:T(8,128)} %rot_hbm.1, f32[2,32,256]{2,1,0:T(8,128)} %read_hbm.1, ...), custom_call_target="tpu_custom_call" | custom-call | tf_op jit(solution)/shard_map/layer/pallas_call | solution.py:424
  59.4 1.0 %finish.1 = (bf16[128,256]{1,0:T(8,128)(2,1)}, bf16[128,256]{1,0:T(8,128)(2,1)}, f32[256,256]{1,0:T(8,128)}, f32[2,32,256]{2,1,0:T(8,128)}, f32[1,256]{1,0:T(1,128)}) custom-call(bf16[128,256]{1,0:T(8,128)(2,1)S(1)} %get-tuple-element.13.out_ref, bf16[128,256]{1,0:T(8,128)(2,1)S(1)} %get-tuple-element.14.ig_ref, f32[2,32,3,4,128]{4,3,2,1,0:T(4,128)S(1)} %get-tuple-element.15.full), custom_call_target="tpu_custom_call" | custom-call | tf_op jit(solution)/shard_map/finish/pallas_call | solution.py:449

commit v3 on v2

--- a/solution.py
+++ b/solution.py
@@ -82,24 +82,31 @@
     lam_s, cof_s, l128, l1024,
     e_buf, o_buf, t_buf, r1f, r2f, hin, r1b, r2b, lin,
     pb, gb, ra1p, ra1g, a2s, ra2, pc, ra3,
-    isem, ssem, rsem,
+    isem, ssem, rsem, near_sem, far_sem,
 ):
     s, b = lax.axis_index("seq"), lax.axis_index("batch")
     g, blk = lax.rem(s, GROUP), lax.div(s, GROUP)
     y, c = lax.div(b, 2), lax.rem(b, 2)
     me = lax.div(g, 4) * 16 + lax.rem(g, 4) * 4 + y
 
-    def in_block(k):
-        return {"seq": blk * GROUP + lax.rem(g + k, GROUP), "batch": b}
-
-    def across(k):
-        return {"seq": lax.rem(blk + k, BLOCKS) * GROUP + g, "batch": b}
-
-    def owner(k):
-        o = lax.rem(me + k, OWNERS)
-        seq = blk * GROUP + lax.div(o, 16) * 4 + lax.div(lax.rem(o, 16), 4)
-        return o, {"seq": seq, "batch": lax.rem(o, 4) * 2 + c}
-
+    base = blk * GROUP
+    zs = [lax.rem(lax.div(g, 4) + k, 2) for k in range(2)]
+    xs = [lax.rem(lax.rem(g, 4) + k, 4) for k in range(4)]
+    ys = [lax.rem(y + k, 4) for k in range(4)]
+    seqs = [[base + z * 4 + x for x in xs] for z in zs]
+    batches = [v * 2 + c for v in ys]
+    in_block = [
+        (zs[k // 4] * 4 + xs[k % 4], {"seq": seqs[k // 4][k % 4], "batch": b})
+        for k in range(1, GROUP)
+    ]
+    across = [{"seq": lax.rem(blk + k, BLOCKS) * GROUP + g, "batch": b} for k in range(BLOCKS)]
+    owners = [
+        (
+            zs[k // 16] * 16 + xs[k // 4 % 4] * 4 + ys[k % 4],
+            {"seq": seqs[k // 16][k // 4 % 4], "batch": batches[k % 4]},
+        )
+        for k in range(1, OWNERS)
+    ]
     other = {"seq": s, "batch": y * 2 + (1 - c)}
 
     fetches = [
@@ -113,11 +120,14 @@
         fetch.start()
 
     barrier = pltpu.get_barrier_semaphore()
-    partners = [across(k) for k in range(1, BLOCKS)]
-    partners += [owner(k)[1] for k in range(1, OWNERS)] + [other]
-    partners_n = len(partners)
-    for device in partners:
-        pl.semaphore_signal(barrier, inc=1, device_id=device, device_id_type=MESH)
+    partners = [device for _, device in in_block] + [across[1], across[7], other]
+    partners += [{"seq": s, "batch": batch} for batch in batches[1:]]
+
+    def greet(sem, devices):
+        for device in devices:
+            pl.semaphore_signal(sem, inc=1, device_id=device, device_id_type=MESH)
+
+    greet(barrier, partners)
 
     def copy(src, dst, n, device):
         return pltpu.make_async_remote_copy(
@@ -140,15 +150,22 @@
     row_id = lax.broadcasted_iota(jnp.int32, (8, CHANNELS), 0)
     zero = jnp.zeros((STATES, CHANNELS), F32)
 
-    def sweep(carry, body, backward=False):
+    def sweep(carry, body, backward=False, lo=0, hi=RUN // 8):
         def step(i, carry):
             first = RUN - 8 - 8 * i if backward else 8 * i
-            first = pl.multiple_of(first, 8)
-            return body(first, carry)
-
-        return lax.fori_loop(0, RUN // 8, step, carry)
+            return body(pl.multiple_of(first, 8), carry)
+
+        return lax.fori_loop(lo, hi, step, carry)
 
     order = tuple(range(8))
+
+    def fwd_state(first, carry):
+        lam_re, lam_im = lam_s[0], lam_s[1]
+        rows = xf[pl.ds(first, 8), :]
+        re, im = carry
+        for j in order:
+            re, im = lam_re * re - lam_im * im + rows[j : j + 1, :], lam_re * im + lam_im * re
+        return re, im
 
     def fwd_local(first, carry):
         lam_re, lam_im = lam_s[0], lam_s[1]
@@ -163,26 +180,22 @@
         mix[pl.ds(first, 8), :] = acc + rows * skip_ref[...]
         return re, im
 
-    re, im = sweep((zero, zero), fwd_local)
+    re, im = sweep((zero, zero), fwd_state)
     put_pieces(e_buf, (gain * re, gain * im))
-    hb[...] = lax.dot_general(
-        cot_ref[...], proj_ref[...], (((1,), (1,)), ((), ())), preferred_element_type=F32
-    )
-    pl.semaphore_wait(barrier, partners_n)
+    pl.semaphore_wait(barrier, len(partners))
 
     sends = []
 
     def scatter(buf, dst, n):
         dst[g] = buf[g]
-        for k in range(1, GROUP):
-            p = lax.rem(g + k, GROUP)
-            copy(buf.at[p], dst.at[g], n, in_block(k)).start()
+        for p, device in in_block:
+            copy(buf.at[p], dst.at[g], n, device).start()
         sends.append((buf.at[pl.ds(0, GROUP - 1)], n))
 
     def spread(src, dst, n):
         dst[blk] = src[...]
-        for k in range(1, BLOCKS):
-            copy(src, dst.at[blk], n, across(k)).start()
+        for k in (4, 5, 3, 6, 2, 7, 1):
+            copy(src, dst.at[blk], n, across[k]).start()
         sends.append((dst.at[pl.ds(0, BLOCKS - 1)], n))
 
     def arrive(ref, n):
@@ -213,6 +226,15 @@
     seven = pl.ds(0, 7)
 
     scatter(e_buf, r1f, 0)
+    greet(near_sem, (across[1], across[7]))
+    state = sweep((zero, zero), fwd_local, hi=RUN // 16)
+    pl.semaphore_wait(near_sem, 2)
+    greet(far_sem, (across[2], across[6]))
+    sweep(state, fwd_local, lo=RUN // 16)
+    hb[...] = lax.dot_general(
+        cot_ref[...], proj_ref[...], (((1,), (1,)), ((), ())), preferred_element_type=F32
+    )
+    pl.semaphore_wait(far_sem, 2)
     arrive(r1f.at[seven], 0)
     t = block_total(r1f, up)
     t_buf[0, 0:8, :], t_buf[0, 8:16, :] = t
@@ -288,24 +310,26 @@
     arrive(ra1p, 3)
     for o in range(OWNERS):
         a2s[o, 0:2] = pb[c, o] + ra1p[o]
-    ra2[me, 0:2] = a2s[me, 0:2]
-    for k in range(1, OWNERS):
-        o, device = owner(k)
-        copy(a2s.at[o, pl.ds(0, 2)], ra2.at[me, pl.ds(0, 2)], 6, device).start()
-    sends.append((ra1p.at[pl.ds(0, OWNERS - 1)], 6))
     arrive(ra1g, 5)
     for o in range(OWNERS):
         a2s[o, 2] = gb[c, o] + ra1g[o]
-    ra2[me, 2] = a2s[me, 2]
-    for k in range(1, OWNERS):
-        o, device = owner(k)
-        copy(a2s.at[o, 2], ra2.at[me, 2], 12, device).start()
-    sends.append((ra1g.at[pl.ds(0, OWNERS - 1)], 12))
+    ra2[me] = a2s[me]
+    for o, device in owners:
+        copy(a2s.at[o], ra2.at[me], 6, device).start()
+    sends.append((ra2.at[pl.ds(0, OWNERS - 1)], 6))
 
     arrive(r1b.at[seven], 4)
     t = block_total(r1b, down)
     t_buf[1, 0:8, :], t_buf[1, 8:16, :] = t
     spread(t_buf.at[1], r2b, 7)
+
+
+    arrive(ra2.at[pl.ds(0, OWNERS - 1)], 6)
+    total = ra2[0]
+    for o in range(1, OWNERS):
+        total = total + ra2[o]
+    pc[0] = total
+    spread(pc.at[0], ra3, 8)
 
     out_ref[...] = (
         xf[...] + jnp.dot(hidden, proj_ref[...], preferred_element_type=F32)
@@ -327,14 +351,6 @@
     sweep((zero, zero), bwd_read, True)
     il[...] = il[...] + cot_ref[...].astype(F32)
 
-    arrive(ra2.at[pl.ds(0, OWNERS - 1), pl.ds(0, 2)], 6)
-    arrive(ra2.at[pl.ds(0, OWNERS - 1), 2], 12)
-    total = ra2[0]
-    for o in range(1, OWNERS):
-        total = total + ra2[o]
-    pc[0] = total
-    spread(pc.at[0], ra3, 8)
-
     arrive(r2b.at[seven], 7)
     entering(r1b, r2b, o_buf.at[1], down, True)
     scatter(o_buf.at[1], lin, 9)
@@ -344,8 +360,8 @@
     for o in range(1, BLOCKS):
         total = total + ra3[o]
     full[c, me] = total
-    for k in range(1, OWNERS):
-        copy(full.at[c, me], full.at[c, me], 10, owner(k)[1]).start()
+    for _, device in owners:
+        copy(full.at[c, me], full.at[c, me], 10, device).start()
     sends.append((ra2.at[pl.ds(0, OWNERS - 1)], 10))
 
     arrive(lin.at[seven], 9)
@@ -432,7 +448,7 @@
         out_specs=[vmem] * 3,
         scratch_shapes=operands
         + [pltpu.VMEM(shape, F32) for shape in shapes]
-        + [pltpu.SemaphoreType.DMA((7,)), pltpu.SemaphoreType.DMA((13,)), pltpu.SemaphoreType.DMA((13,))],
+        + [pltpu.SemaphoreType.DMA((7,)), pltpu.SemaphoreType.DMA((12,)), pltpu.SemaphoreType.DMA((12,)), pltpu.SemaphoreType.REGULAR, pltpu.SemaphoreType.REGULAR],
         compiler_params=pltpu.CompilerParams(
             collective_id=0, has_side_effects=True, vmem_limit_bytes=32 << 20
         ),

time: 60.6 us -> 58.4 us (0.964)
  Pallas kernels: 59.8 us -> 57.6 us
    pallas_call x1, Pallas kernels: 58.8 us -> 56.6 us  [shards(): pl.pallas_call(kernel, out_shape=(jax.ShapeDtypeStruct(row, bf16), jax.Sh...]
where the time goes in v3:
time: 58.4 us; the launch traced here: 58.2 us
  Pallas kernels  57.6 us (99%)
  between operations  0.64 us (1%)
    pallas_call x1, Pallas kernels, shards(): pl.pallas_call(kernel, out_shape=(jax.ShapeDtypeStruct(row, bf16), jax.Sh...  56.6 us

profile of v3, /device:TPU:1, one launch (start us, length us, event | category | flops | bytes accessed | tf_op | source)
XLA Modules:
  0.0 58.2 jit_solution(8312427365602116159)
XLA Ops:
  0.6 56.6 %layer.1 = (bf16[128,256]{1,0:T(8,128)(2,1)S(1)}, bf16[128,256]{1,0:T(8,128)(2,1)S(1)}, f32[2,32,3,4,128]{4,3,2,1,0:T(4,128)S(1)}) custom-call(bf16[128,256]{1,0:T(8,128)(2,1)} %bitcast.6, bf16[128,256]{1,0:T(8,128)(2,1)} %bitcast.7, f32[32,256]{1,0:T(8,128)} %decay_hbm.1, f32[32,256]{1,0:T(8,128)} %rot_hbm.1, f32[2,32,256]{2,1,0:T(8,128)} %read_hbm.1, ...), custom_call_target="tpu_custom_call" | custom-call | tf_op jit(solution)/shard_map/layer/pallas_call | solution.py:440
  57.2 1.0 %finish.1 = (bf16[128,256]{1,0:T(8,128)(2,1)}, bf16[128,256]{1,0:T(8,128)(2,1)}, f32[256,256]{1,0:T(8,128)}, f32[2,32,256]{2,1,0:T(8,128)}, f32[1,256]{1,0:T(1,128)}) custom-call(bf16[128,256]{1,0:T(8,128)(2,1)S(1)} %get-tuple-element.13.out_ref, bf16[128,256]{1,0:T(8,128)(2,1)S(1)} %get-tuple-element.14.ig_ref, f32[2,32,3,4,128]{4,3,2,1,0:T(4,128)S(1)} %get-tuple-element.15.full), custom_call_target="tpu_custom_call" | custom-call | tf_op jit(solution)/shard_map/finish/pallas_call | solution.py:465

commit v4 on v3

--- a/solution.py
+++ b/solution.py
@@ -79,10 +79,10 @@
     out_ref, ig_ref, full,
     x_ref, cot_ref, decay_ref, rot_ref, read_ref, skip_ref, proj_ref,
     xf, gf, mix, hb, il,
-    lam_s, cof_s, l128, l1024,
+    tab, lam_s, cof_s, l128, l1024,
     e_buf, o_buf, t_buf, r1f, r2f, hin, r1b, r2b, lin,
     pb, gb, ra1p, ra1g, a2s, ra2, pc, ra3,
-    isem, ssem, rsem, near_sem, far_sem,
+    isem, ssem, rsem, far_sem,
 ):
     s, b = lax.axis_index("seq"), lax.axis_index("batch")
     g, blk = lax.rem(s, GROUP), lax.div(s, GROUP)
@@ -120,7 +120,7 @@
         fetch.start()
 
     barrier = pltpu.get_barrier_semaphore()
-    partners = [device for _, device in in_block] + [across[1], across[7], other]
+    partners = [device for _, device in in_block] + [across[k] for k in (1, 2, 6, 7)] + [other]
     partners += [{"seq": s, "batch": batch} for batch in batches[1:]]
 
     def greet(sem, devices):
@@ -225,12 +225,9 @@
     up, down = tuple(range(8)), tuple(range(7, -1, -1))
     seven = pl.ds(0, 7)
 
+    greet(far_sem, (across[2], across[6]))
     scatter(e_buf, r1f, 0)
-    greet(near_sem, (across[1], across[7]))
-    state = sweep((zero, zero), fwd_local, hi=RUN // 16)
-    pl.semaphore_wait(near_sem, 2)
-    greet(far_sem, (across[2], across[6]))
-    sweep(state, fwd_local, lo=RUN // 16)
+    sweep((zero, zero), fwd_local)
     hb[...] = lax.dot_general(
         cot_ref[...], proj_ref[...], (((1,), (1,)), ((), ())), preferred_element_type=F32
     )
@@ -239,6 +236,14 @@
     t = block_total(r1f, up)
     t_buf[0, 0:8, :], t_buf[0, 8:16, :] = t
     spread(t_buf.at[0], r2f, 1)
+
+    def fill_table(j, power):
+        tab[j, 0], tab[j, 1] = power
+        return cmul((lam_s[0], lam_s[1]), power)
+
+    lax.fori_loop(0, 16, fill_table, (lam_s[0], lam_s[1]))
+    gb[...] = jnp.zeros_like(gb)
+    a2s[...] = jnp.zeros_like(a2s)
     arrive(r2f.at[seven], 1)
     entering(r1f, r2f, o_buf.at[0], up, False)
     scatter(o_buf.at[0], hin, 2)
@@ -247,17 +252,23 @@
     enter = get_pieces(hin)
     carried = cmul((read_ref[0], read_ref[1]), enter)
 
-    def fwd_inject(first, carry):
-        lam_re, lam_im = lam_s[0], lam_s[1]
-        re, im = carry
-        acc = jnp.zeros((8, CHANNELS), F32)
-        for j in order:
-            re, im = lam_re * re - lam_im * im, lam_re * im + lam_im * re
-            acc = jnp.where(row_id == j, jnp.sum(re, axis=0, keepdims=True), acc)
-        mix[pl.ds(first, 8), :] = mix[pl.ds(first, 8), :] + acc
-        return re, im
-
-    sweep(carried, fwd_inject)
+    def inject(carried, ref, backward):
+        def step(i, carry):
+            re, im = carry
+            for part in range(2):
+                first = 16 * i + 8 * part
+                acc = jnp.zeros((8, CHANNELS), F32)
+                for j in order:
+                    n = 8 * part + j
+                    total = jnp.sum(tab[n, 0] * re - tab[n, 1] * im, axis=0, keepdims=True)
+                    acc = jnp.where(row_id == (7 - j if backward else j), total, acc)
+                first = pl.multiple_of(RUN - 8 - first if backward else first, 8)
+                ref[pl.ds(first, 8), :] = ref[pl.ds(first, 8), :] + acc
+            return cmul((tab[15, 0], tab[15, 1]), carry)
+
+        lax.fori_loop(0, RUN // 16, step, carried)
+
+    inject(carried, mix, False)
 
     mixed = mix[...]
     square = mixed * mixed
@@ -298,25 +309,27 @@
     read_re = gain * sum_re + extra[0]
     read_im = -(gain * sum_im + extra[1])
     skip_part = jnp.sum(gf[...] * xf[...], axis=0, keepdims=True)
-    gb[...] = jnp.zeros_like(gb)
     for half_id in range(2):
         cols = slice(128 * half_id, 128 * half_id + 128)
-        for o in range(OWNERS):
-            rows = (read_re if o < 16 else read_im)[2 * (o % 16) : 2 * (o % 16) + 2, cols]
-            gb[half_id, o, 0:2, :] = rows
-        gb[half_id, 0, 2:3, :] = skip_part[:, cols]
+        for o in range(16):
+            gb[half_id, o] = (read_re if o < 8 else read_im)[4 * (o % 8) : 4 * (o % 8) + 4, cols]
+        gb[half_id, 16, 0:1, :] = skip_part[:, cols]
     copy(gb.at[1 - c], ra1g, 5, other).start()
     sends.append((gb.at[0], 5))
     arrive(ra1p, 3)
     for o in range(OWNERS):
         a2s[o, 0:2] = pb[c, o] + ra1p[o]
+    ra2[me, 0:2] = a2s[me, 0:2]
+    for o, device in owners:
+        copy(a2s.at[o, pl.ds(0, 2)], ra2.at[me, pl.ds(0, 2)], 6, device).start()
+    sends.append((ra1p.at[pl.ds(0, OWNERS - 1)], 6))
     arrive(ra1g, 5)
-    for o in range(OWNERS):
+    for o in range(17):
         a2s[o, 2] = gb[c, o] + ra1g[o]
-    ra2[me] = a2s[me]
+    ra2[me, 2] = a2s[me, 2]
     for o, device in owners:
-        copy(a2s.at[o], ra2.at[me], 6, device).start()
-    sends.append((ra2.at[pl.ds(0, OWNERS - 1)], 6))
+        copy(a2s.at[o, 2], ra2.at[me, 2], 12, device).start()
+    sends.append((ra2.at[pl.ds(0, OWNERS - 1), 2], 12))
 
     arrive(r1b.at[seven], 4)
     t = block_total(r1b, down)
@@ -324,7 +337,8 @@
     spread(t_buf.at[1], r2b, 7)
 
 
-    arrive(ra2.at[pl.ds(0, OWNERS - 1)], 6)
+    arrive(ra2.at[pl.ds(0, OWNERS - 1), pl.ds(0, 2)], 6)
+    arrive(ra2.at[pl.ds(0, OWNERS - 1), 2], 12)
     total = ra2[0]
     for o in range(1, OWNERS):
         total = total + ra2[o]
@@ -367,17 +381,7 @@
     arrive(lin.at[seven], 9)
     carried = cmul((cof_s[0], cof_s[1]), get_pieces(lin))
 
-    def bwd_inject(first, carry):
-        lam_re, lam_im = lam_s[0], lam_s[1]
-        re, im = carry
-        acc = jnp.zeros((8, CHANNELS), F32)
-        for j in reversed(order):
-            re, im = lam_re * re - lam_im * im, lam_re * im + lam_im * re
-            acc = jnp.where(row_id == j, jnp.sum(re, axis=0, keepdims=True), acc)
-        il[pl.ds(first, 8), :] = il[pl.ds(first, 8), :] + acc
-        return re, im
-
-    sweep(carried, bwd_inject, True)
+    inject(carried, il, True)
     ig_ref[...] = il[...].astype(jnp.bfloat16)
 
     arrive(full.at[c, pl.ds(0, OWNERS - 1)], 10)
@@ -413,9 +417,10 @@
             for q in range(2):
                 row = 8 * o + 4 * q
                 pg_ref[row : row + 4, cols] = full[half_id, o, q] * factor
-            row = 2 * (o % 16)
-            rg_ref[o // 16, row : row + 2, cols] = full[half_id, o, 2, 0:2, :] * factor
-        sg_ref[:, cols] = full[half_id, 0, 2, 2:3, :] * factor
+        for o in range(16):
+            row = 4 * (o % 8)
+            rg_ref[o // 8, row : row + 4, cols] = full[half_id, o, 2] * factor
+        sg_ref[:, cols] = full[half_id, 16, 2, 0:1, :] * factor
     writes += [write(pg_ref, pg_hbm, 2), write(rg_ref, rg_hbm, 3), write(sg_ref, sg_hbm, 4)]
     for done in writes:
         done.wait()
@@ -433,9 +438,9 @@
         pltpu.VMEM(state[1:], F32), pltpu.VMEM(state, F32), pltpu.VMEM((1, CHANNELS), F32),
         pltpu.VMEM(square, bf16),
     ]
-    shapes = [row] * 5 + [state, state, pieces, pieces]
+    shapes = [row] * 5 + [(16,) + state, state, state, pieces, pieces]
     shapes += [(2 * GROUP, 16, 128), (2,) + pieces, (2, 16, 128)] + [pieces] * 6
-    shapes += [(2, OWNERS, 2, 4, 128), (2, OWNERS, 4, 128), (OWNERS, 2, 4, 128), (OWNERS, 4, 128)]
+    shapes += [(2, OWNERS, 2, 4, 128), (2, 17, 4, 128), (OWNERS, 2, 4, 128), (17, 4, 128)]
     shapes += [sums[1:], sums[1:], (1, 3, 4, 128), (BLOCKS, 3, 4, 128)]
     out, in_grad, total = pl.pallas_call(
         kernel,
@@ -448,7 +453,7 @@
         out_specs=[vmem] * 3,
         scratch_shapes=operands
         + [pltpu.VMEM(shape, F32) for shape in shapes]
-        + [pltpu.SemaphoreType.DMA((7,)), pltpu.SemaphoreType.DMA((12,)), pltpu.SemaphoreType.DMA((12,)), pltpu.SemaphoreType.REGULAR, pltpu.SemaphoreType.REGULAR],
+        + [pltpu.SemaphoreType.DMA((7,)), pltpu.SemaphoreType.DMA((13,)), pltpu.SemaphoreType.DMA((13,)), pltpu.SemaphoreType.REGULAR],
         compiler_params=pltpu.CompilerParams(
             collective_id=0, has_side_effects=True, vmem_limit_bytes=32 << 20
         ),

time: 58.4 us -> 56.2 us (0.962)
  Pallas kernels: 57.6 us -> 55.4 us
    pallas_call x1, Pallas kernels: 56.6 us -> 54.4 us  [shards(): pl.pallas_call(kernel, out_shape=(jax.ShapeDtypeStruct(row, bf16), jax.Sh...]
where the time goes in v4:
time: 56.2 us; the launch traced here: 56.1 us
  Pallas kernels  55.4 us (99%)
  between operations  0.64 us (1%)
    pallas_call x1, Pallas kernels, shards(): pl.pallas_call(kernel, out_shape=(jax.ShapeDtypeStruct(row, bf16), jax.Sh...  54.4 us

profile of v4, /device:TPU:1, one launch (start us, length us, event | category | flops | bytes accessed | tf_op | source)
XLA Modules:
  0.0 56.1 jit_solution(11016537539226763809)
XLA Ops:
  0.6 54.4 %layer.1 = (bf16[128,256]{1,0:T(8,128)(2,1)S(1)}, bf16[128,256]{1,0:T(8,128)(2,1)S(1)}, f32[2,32,3,4,128]{4,3,2,1,0:T(4,128)S(1)}) custom-call(bf16[128,256]{1,0:T(8,128)(2,1)} %bitcast.6, bf16[128,256]{1,0:T(8,128)(2,1)} %bitcast.7, f32[32,256]{1,0:T(8,128)} %decay_hbm.1, f32[32,256]{1,0:T(8,128)} %rot_hbm.1, f32[2,32,256]{2,1,0:T(8,128)} %read_hbm.1, ...), custom_call_target="tpu_custom_call" | custom-call | tf_op jit(solution)/shard_map/layer/pallas_call | solution.py:445
  55.1 1.0 %finish.1 = (bf16[128,256]{1,0:T(8,128)(2,1)}, bf16[128,256]{1,0:T(8,128)(2,1)}, f32[256,256]{1,0:T(8,128)}, f32[2,32,256]{2,1,0:T(8,128)}, f32[1,256]{1,0:T(1,128)}) custom-call(bf16[128,256]{1,0:T(8,128)(2,1)S(1)} %get-tuple-element.13.out_ref, bf16[128,256]{1,0:T(8,128)(2,1)S(1)} %get-tuple-element.14.ig_ref, f32[2,32,3,4,128]{4,3,2,1,0:T(4,128)S(1)} %get-tuple-element.15.full), custom_call_target="tpu_custom_call" | custom-call | tf_op jit(solution)/shard_map/finish/pallas_call | solution.py:470

commit v5 on v4

--- a/solution.py
+++ b/solution.py
@@ -21,6 +21,13 @@
 GELU_SCALE = math.sqrt(2 / math.pi)
 GELU_CUBE = 0.044715
 CEILING = math.sqrt(CHANNELS * CHANNELS + 2 * STATES * CHANNELS + CHANNELS)
+
+
+def hops(k):
+    return k // 16 + min(k // 4 % 4, 4 - k // 4 % 4) + min(k % 4, 4 - k % 4)
+
+
+FAR_FIRST = sorted(range(1, OWNERS), key=lambda k: (-hops(k), k))
 
 
 def cmul(a, b):
@@ -97,7 +104,7 @@
     batches = [v * 2 + c for v in ys]
     in_block = [
         (zs[k // 4] * 4 + xs[k % 4], {"seq": seqs[k // 4][k % 4], "batch": b})
-        for k in range(1, GROUP)
+        for k in (6, 5, 7, 2, 4, 1, 3)
     ]
     across = [{"seq": lax.rem(blk + k, BLOCKS) * GROUP + g, "batch": b} for k in range(BLOCKS)]
     owners = [
@@ -105,7 +112,7 @@
             zs[k // 16] * 16 + xs[k // 4 % 4] * 4 + ys[k % 4],
             {"seq": seqs[k // 16][k // 4 % 4], "batch": batches[k % 4]},
         )
-        for k in range(1, OWNERS)
+        for k in FAR_FIRST
     ]
     other = {"seq": s, "batch": y * 2 + (1 - c)}
 
@@ -120,8 +127,8 @@
         fetch.start()
 
     barrier = pltpu.get_barrier_semaphore()
-    partners = [device for _, device in in_block] + [across[k] for k in (1, 2, 6, 7)] + [other]
-    partners += [{"seq": s, "batch": batch} for batch in batches[1:]]
+    partners = [across[k] for k in (2, 6, 1, 7)] + [device for _, device in in_block]
+    partners += [{"seq": s, "batch": batch} for batch in batches[1:]] + [other]
 
     def greet(sem, devices):
         for device in devices:
@@ -302,8 +309,6 @@
         return re, im, sum_re, sum_im
 
     re, im, sum_re, sum_im = sweep((zero, zero, zero, zero), bwd_local, True)
-    put_pieces(e_buf.at[pl.ds(GROUP, GROUP)], (re, im))
-    scatter(e_buf.at[pl.ds(GROUP, GROUP)], r1b, 4)
     lam = lam_s[0], lam_s[1]
     extra = cmul(cmul(lam, (re, im)), get_pieces(hin))
     read_re = gain * sum_re + extra[0]
@@ -316,6 +321,8 @@
         gb[half_id, 16, 0:1, :] = skip_part[:, cols]
     copy(gb.at[1 - c], ra1g, 5, other).start()
     sends.append((gb.at[0], 5))
+    put_pieces(e_buf.at[pl.ds(GROUP, GROUP)], (re, im))
+    scatter(e_buf.at[pl.ds(GROUP, GROUP)], r1b, 4)
     arrive(ra1p, 3)
     for o in range(OWNERS):
         a2s[o, 0:2] = pb[c, o] + ra1p[o]
@@ -339,10 +346,10 @@
 
     arrive(ra2.at[pl.ds(0, OWNERS - 1), pl.ds(0, 2)], 6)
     arrive(ra2.at[pl.ds(0, OWNERS - 1), 2], 12)
-    total = ra2[0]
-    for o in range(1, OWNERS):
-        total = total + ra2[o]
-    pc[0] = total
+    terms = [ra2[o] for o in range(OWNERS)]
+    while len(terms) > 1:
+        terms = [a + b for a, b in zip(terms[::2], terms[1::2])]
+    pc[0] = terms[0]
     spread(pc.at[0], ra3, 8)
 
     out_ref[...] = (

time: 56.2 us -> 55 us (0.979)
  Pallas kernels: 55.4 us -> 54.2 us
    pallas_call x1, Pallas kernels: 54.4 us -> 53.2 us  [shards(): pl.pallas_call(kernel, out_shape=(jax.ShapeDtypeStruct(row, bf16), jax.Sh...]
where the time goes in v5:
time: 55 us; the launch traced here: 54.8 us
  Pallas kernels  54.2 us (99%)
  between operations  0.64 us (1%)
    pallas_call x1, Pallas kernels, shards(): pl.pallas_call(kernel, out_shape=(jax.ShapeDtypeStruct(row, bf16), jax.Sh...  53.2 us

profile of v5, /device:TPU:1, one launch (start us, length us, event | category | flops | bytes accessed | tf_op | source)
XLA Modules:
  0.0 54.8 jit_solution(3704782030525302692)
XLA Ops:
  0.6 53.2 %layer.1 = (bf16[128,256]{1,0:T(8,128)(2,1)S(1)}, bf16[128,256]{1,0:T(8,128)(2,1)S(1)}, f32[2,32,3,4,128]{4,3,2,1,0:T(4,128)S(1)}) custom-call(bf16[128,256]{1,0:T(8,128)(2,1)} %bitcast.6, bf16[128,256]{1,0:T(8,128)(2,1)} %bitcast.7, f32[32,256]{1,0:T(8,128)} %decay_hbm.1, f32[32,256]{1,0:T(8,128)} %rot_hbm.1, f32[2,32,256]{2,1,0:T(8,128)} %read_hbm.1, ...), custom_call_target="tpu_custom_call" | custom-call | tf_op jit(solution)/shard_map/layer/pallas_call | solution.py:452
  53.8 1.0 %finish.1 = (bf16[128,256]{1,0:T(8,128)(2,1)}, bf16[128,256]{1,0:T(8,128)(2,1)}, f32[256,256]{1,0:T(8,128)}, f32[2,32,256]{2,1,0:T(8,128)}, f32[1,256]{1,0:T(1,128)}) custom-call(bf16[128,256]{1,0:T(8,128)(2,1)S(1)} %get-tuple-element.13.out_ref, bf16[128,256]{1,0:T(8,128)(2,1)S(1)} %get-tuple-element.14.ig_ref, f32[2,32,3,4,128]{4,3,2,1,0:T(4,128)S(1)} %get-tuple-element.15.full), custom_call_target="tpu_custom_call" | custom-call | tf_op jit(solution)/shard_map/finish/pallas_call | solution.py:477

commit v6 on v5

--- a/solution.py
+++ b/solution.py
@@ -326,17 +326,13 @@
     arrive(ra1p, 3)
     for o in range(OWNERS):
         a2s[o, 0:2] = pb[c, o] + ra1p[o]
-    ra2[me, 0:2] = a2s[me, 0:2]
-    for o, device in owners:
-        copy(a2s.at[o, pl.ds(0, 2)], ra2.at[me, pl.ds(0, 2)], 6, device).start()
-    sends.append((ra1p.at[pl.ds(0, OWNERS - 1)], 6))
     arrive(ra1g, 5)
     for o in range(17):
         a2s[o, 2] = gb[c, o] + ra1g[o]
-    ra2[me, 2] = a2s[me, 2]
+    ra2[me] = a2s[me]
     for o, device in owners:
-        copy(a2s.at[o, 2], ra2.at[me, 2], 12, device).start()
-    sends.append((ra2.at[pl.ds(0, OWNERS - 1), 2], 12))
+        copy(a2s.at[o], ra2.at[me], 6, device).start()
+    sends.append((ra2.at[pl.ds(0, OWNERS - 1)], 6))
 
     arrive(r1b.at[seven], 4)
     t = block_total(r1b, down)
@@ -344,8 +340,7 @@
     spread(t_buf.at[1], r2b, 7)
 
 
-    arrive(ra2.at[pl.ds(0, OWNERS - 1), pl.ds(0, 2)], 6)
-    arrive(ra2.at[pl.ds(0, OWNERS - 1), 2], 12)
+    arrive(ra2.at[pl.ds(0, OWNERS - 1)], 6)
     terms = [ra2[o] for o in range(OWNERS)]
     while len(terms) > 1:
         terms = [a + b for a, b in zip(terms[::2], terms[1::2])]
@@ -382,7 +377,10 @@
         total = total + ra3[o]
     full[c, me] = total
     for _, device in owners:
+        far = {"seq": device["seq"], "batch": device["batch"] + (1 - 2 * c)}
+        copy(full.at[c, me], full.at[c, me], 11, far).start()
         copy(full.at[c, me], full.at[c, me], 10, device).start()
+    copy(full.at[c, me], full.at[c, me], 11, other).start()
     sends.append((ra2.at[pl.ds(0, OWNERS - 1)], 10))
 
     arrive(lin.at[seven], 9)
@@ -392,7 +390,6 @@
     ig_ref[...] = il[...].astype(jnp.bfloat16)
 
     arrive(full.at[c, pl.ds(0, OWNERS - 1)], 10)
-    copy(full.at[c], full.at[c], 11, other).start()
     sends.append((full.at[0], 11))
     arrive(full.at[1 - c], 11)
     for ref, n in sends:
@@ -460,7 +457,7 @@
         out_specs=[vmem] * 3,
         scratch_shapes=operands
         + [pltpu.VMEM(shape, F32) for shape in shapes]
-        + [pltpu.SemaphoreType.DMA((7,)), pltpu.SemaphoreType.DMA((13,)), pltpu.SemaphoreType.DMA((13,)), pltpu.SemaphoreType.REGULAR],
+        + [pltpu.SemaphoreType.DMA((7,)), pltpu.SemaphoreType.DMA((12,)), pltpu.SemaphoreType.DMA((12,)), pltpu.SemaphoreType.REGULAR],
         compiler_params=pltpu.CompilerParams(
             collective_id=0, has_side_effects=True, vmem_limit_bytes=32 << 20
         ),

time: 55 us -> 54.4 us (0.989)
  Pallas kernels: 54.2 us -> 53.6 us
    pallas_call x1, Pallas kernels: 53.2 us -> 52.6 us  [shards(): pl.pallas_call(kernel, out_shape=(jax.ShapeDtypeStruct(row, bf16), jax.Sh...]
where the time goes in v6:
time: 54.4 us; the launch traced here: 54.3 us
  Pallas kernels  53.6 us (99%)
  between operations  0.64 us (1%)
    pallas_call x1, Pallas kernels, shards(): pl.pallas_call(kernel, out_shape=(jax.ShapeDtypeStruct(row, bf16), jax.Sh...  52.6 us

profile of v6, /device:TPU:1, one launch (start us, length us, event | category | flops | bytes accessed | tf_op | source)
XLA Modules:
  0.0 54.3 jit_solution(8912339261064951248)
XLA Ops:
  0.6 52.6 %layer.1 = (bf16[128,256]{1,0:T(8,128)(2,1)S(1)}, bf16[128,256]{1,0:T(8,128)(2,1)S(1)}, f32[2,32,3,4,128]{4,3,2,1,0:T(4,128)S(1)}) custom-call(bf16[128,256]{1,0:T(8,128)(2,1)} %bitcast.6, bf16[128,256]{1,0:T(8,128)(2,1)} %bitcast.7, f32[32,256]{1,0:T(8,128)} %decay_hbm.1, f32[32,256]{1,0:T(8,128)} %rot_hbm.1, f32[2,32,256]{2,1,0:T(8,128)} %read_hbm.1, ...), custom_call_target="tpu_custom_call" | custom-call | tf_op jit(solution)/shard_map/layer/pallas_call | solution.py:449
  53.3 1.0 %finish.1 = (bf16[128,256]{1,0:T(8,128)(2,1)}, bf16[128,256]{1,0:T(8,128)(2,1)}, f32[256,256]{1,0:T(8,128)}, f32[2,32,256]{2,1,0:T(8,128)}, f32[1,256]{1,0:T(1,128)}) custom-call(bf16[128,256]{1,0:T(8,128)(2,1)S(1)} %get-tuple-element.13.out_ref, bf16[128,256]{1,0:T(8,128)(2,1)S(1)} %get-tuple-element.14.ig_ref, f32[2,32,3,4,128]{4,3,2,1,0:T(4,128)S(1)} %get-tuple-element.15.full), custom_call_target="tpu_custom_call" | custom-call | tf_op jit(solution)/shard_map/finish/pallas_call | solution.py:474

commit v7 on v6

--- a/solution.py
+++ b/solution.py
@@ -123,9 +123,6 @@
              (skip_hbm, skip_ref), (cot_hbm, cot_ref), (proj_hbm, proj_ref)]
         )
     ]
-    for fetch in fetches:
-        fetch.start()
-
     barrier = pltpu.get_barrier_semaphore()
     partners = [across[k] for k in (2, 6, 1, 7)] + [device for _, device in in_block]
     partners += [{"seq": s, "batch": batch} for batch in batches[1:]] + [other]
@@ -135,6 +132,8 @@
             pl.semaphore_signal(sem, inc=1, device_id=device, device_id_type=MESH)
 
     greet(barrier, partners)
+    for fetch in fetches:
+        fetch.start()
 
     def copy(src, dst, n, device):
         return pltpu.make_async_remote_copy(
@@ -148,8 +147,6 @@
     decay, rot = decay_ref[...], rot_ref[...]
     gain = entry_gain(decay)
     lam = decay_power(decay, rot, 1)
-    put_pieces(l128, decay_power(decay, rot, RUN))
-    put_pieces(l1024, decay_power(decay, rot, RUN * GROUP))
     lam_s[0], lam_s[1] = lam
     cof_s[0] = gain * read_ref[0]
     cof_s[1] = gain * read_ref[1]
@@ -234,6 +231,8 @@
 
     greet(far_sem, (across[2], across[6]))
     scatter(e_buf, r1f, 0)
+    put_pieces(l128, decay_power(decay, rot, RUN))
+    put_pieces(l1024, decay_power(decay, rot, RUN * GROUP))
     sweep((zero, zero), fwd_local)
     hb[...] = lax.dot_general(
         cot_ref[...], proj_ref[...], (((1,), (1,)), ((), ())), preferred_element_type=F32

time: 54.4 us -> 54.4 us (level)
  no operation moved by 1% of the time
where the time goes in v7:
time: 54.4 us; the launch traced here: 54.3 us
  Pallas kernels  53.6 us (99%)
  between operations  0.64 us (1%)
    pallas_call x1, Pallas kernels, shards(): pl.pallas_call(kernel, out_shape=(jax.ShapeDtypeStruct(row, bf16), jax.Sh...  52.7 us

profile of v7, /device:TPU:1, one launch (start us, length us, event | category | flops | bytes accessed | tf_op | source)
XLA Modules:
  0.0 54.3 jit_solution(12692087745760575663)
XLA Ops:
  0.6 52.7 %layer.1 = (bf16[128,256]{1,0:T(8,128)(2,1)S(1)}, bf16[128,256]{1,0:T(8,128)(2,1)S(1)}, f32[2,32,3,4,128]{4,3,2,1,0:T(4,128)S(1)}) custom-call(bf16[128,256]{1,0:T(8,128)(2,1)} %bitcast.6, bf16[128,256]{1,0:T(8,128)(2,1)} %bitcast.7, f32[32,256]{1,0:T(8,128)} %decay_hbm.1, f32[32,256]{1,0:T(8,128)} %rot_hbm.1, f32[2,32,256]{2,1,0:T(8,128)} %read_hbm.1, ...), custom_call_target="tpu_custom_call" | custom-call | tf_op jit(solution)/shard_map/layer/pallas_call | solution.py:448
  53.3 1.0 %finish.1 = (bf16[128,256]{1,0:T(8,128)(2,1)}, bf16[128,256]{1,0:T(8,128)(2,1)}, f32[256,256]{1,0:T(8,128)}, f32[2,32,256]{2,1,0:T(8,128)}, f32[1,256]{1,0:T(1,128)}) custom-call(bf16[128,256]{1,0:T(8,128)(2,1)S(1)} %get-tuple-element.13.out_ref, bf16[128,256]{1,0:T(8,128)(2,1)S(1)} %get-tuple-element.14.ig_ref, f32[2,32,3,4,128]{4,3,2,1,0:T(4,128)S(1)} %get-tuple-element.15.full), custom_call_target="tpu_custom_call" | custom-call | tf_op jit(solution)/shard_map/finish/pallas_call | solution.py:473
